TPU v7x, 256 devices: a whole 4x4x8 slice. The times are simulated.
256 devices in a mesh: seq: 32 (over y, z_lo, core), exp: 8 (over z_hi, x).
Axes of the slice: x: 4, y: 4, z: 8 (z_hi: 2, z_lo: 4; z = z_hi * 4 + z_lo), core: 2. Of those that a mesh axis runs over, the one named last changes fastest.
Arguments:
- hidden_in: bfloat16 [24, 6144], P('exp', 'seq'), may hold values from -2 to 2
- queries: bfloat16 [24, 6144], P(None, 'exp'), may hold values from -40 to 40
- key_cache: bfloat16 [24, 8192, 1024], P(None, 'seq', 'exp'), may hold values from -16 to 16
- value_cache: bfloat16 [24, 8192, 1024], P(None, 'seq', 'exp'), may hold values from -6 to 6
- lengths: int32 [24], replicated, may hold values from 2 to 8192
- out_weight: bfloat16 [6144, 6144], P('exp', 'seq'), may hold values from -0.078125 to 0.078125
- norm_gain: float32 [6144], P('seq'), may hold values from 0.1 to 1.9
- router: bfloat16 [6144, 8], P('seq'), may hold values from -0.078125 to 0.078125
- expert_ids: int32 [24, 2], P('exp'), may hold values from 0 to 7, as said below
- capacity: int32 [8], replicated, may hold values from 1 to 3, as said below
- w_gate: bfloat16 [8, 6144, 8192], P('exp', None, 'seq'), may hold values from -0.078125 to 0.078125
- w_up: bfloat16 [8, 6144, 8192], P('exp', None, 'seq'), may hold values from -0.078125 to 0.078125
- w_down: bfloat16 [8, 8192, 6144], P('exp', 'seq'), may hold values from -0.125 to 0.125
Outputs:
- layer_out: bfloat16 [24, 6144], P('exp', 'seq')
Inputs may be any that keep to these rules, and one draw needn't show every extreme that they name: lengths[b] counts sequence b's live cache positions, the newest token's included. `expert_ids`: the two experts of a token differ. One expert is named by every token; any other expert is named at most 3 times within one aligned block of 3 tokens. The expert that every token names has capacity 3.
All inputs are finite; a program needn't handle non-finite values.
Results may differ from a plain program's by a relative error of at most 0.0085.
Values may be sent and summed in bfloat16 or wider, within the bound.
No kernel may reach another device: no remote copies, remote signals or barrier semaphores. Data moves between devices by JAX's collectives and lax.ppermute only.
A program may use at most 64 MiB of HBM per device.

v0:
```python
import math

import jax
import jax.numpy as jnp
from jax import lax
from jax.sharding import Mesh
from jax.sharding import PartitionSpec as P

D = 6144
HEADS = 48
KV_HEADS = 8
HEAD_DIM = 128
EXPERTS = 8
SEQ = ("seq_0", "seq_1", "seq_2")


masked_score = -1e30
norm_eps = 1e-05


def collected_together(value, axis):
    leaves = jax.tree.leaves(value)
    sequence = sorted(range(len(leaves)), key=lambda k: -leaves[k].size)
    width = (1, *leaves[sequence[0]].shape)[-1]
    lines = [
        jnp.pad(leaves[k].reshape(-1), (0, -leaves[k].size % width)).reshape(-1, width)
        for k in sequence
    ]
    both, at, found = (lax.all_gather(jnp.concatenate(lines), axis), 0, {})
    for k, line in zip(sequence, lines):
        share = both[:, at : at + len(line)].reshape(len(both), -1)
        found[k] = share[:, : leaves[k].size].reshape(-1, *leaves[k].shape)
        at += len(line)
    numbers = iter(range(len(leaves)))
    return jax.tree.map(lambda _: found[next(numbers)], value)


def joined_all(value, axes, combine):
    for axis in axes:
        pieces = collected_together(value, axis)
        value = jax.tree.map(lambda part: part[0], pieces)
        for k in range(1, lax.axis_size(axis)):
            value = combine(value, jax.tree.map(lambda part: part[k], pieces))
    return value


def split_up(value, dim, devices):
    before, after = (value.shape[:dim], value.shape[dim + 1 :])
    return jnp.moveaxis(value.reshape(*before, devices, -1, *after), dim, 0)


def sent_and_summed(value, axis, dim):
    pieces = split_up(value, dim, lax.axis_size(axis))
    arrived = lax.all_to_all(pieces, axis, split_axis=0, concat_axis=0, tiled=True)
    return arrived.sum(axis=0)


def copy_for_each(value, axis):
    devices = lax.axis_size(axis)
    return lax.all_to_all(
        jnp.broadcast_to(value[None], (devices, *value.shape)), axis, 0, 0, tiled=True
    )


def of_everyone(value, axis):
    return copy_for_each(value, axis).sum(axis=0)


def packed_total(arrays, axis):
    ends = [0]
    for a in arrays:
        ends.append(ends[-1] + a.size)
    running = of_everyone(jnp.concatenate([a.ravel() for a in arrays]), axis)
    return tuple((running[b:e].reshape(a.shape) for a, b, e in zip(arrays, ends, ends[1:])))


def in_order(pieces, dim):
    shape = list(pieces.shape[1:])
    shape[dim] *= pieces.shape[0]
    return jnp.moveaxis(pieces, 0, dim).reshape(shape)


def gathered_copies(value, axis, dim):
    return in_order(copy_for_each(value, axis), dim)


def merge_partial_results(left_part, right_part):
    left_maximum_score, left_denom, left_sum = left_part
    right_peak, right_denom, right_sum = right_part
    joint_peak = jnp.maximum(left_maximum_score, right_peak)
    left_factor = jnp.exp(left_maximum_score - joint_peak)
    right_factor = jnp.exp(right_peak - joint_peak)
    return (
        joint_peak,
        left_denom * left_factor + right_denom * right_factor,
        left_sum * left_factor[..., None] + right_sum * right_factor[..., None],
    )


def on_device(
    hidden_in,
    queries,
    key_cache,
    value_cache,
    lengths,
    out_weight,
    norm_gain,
    router,
    expert_ids,
    capacity,
    w_gate,
    w_up,
    w_down,
):
    seq_count = queries.shape[0]
    group_size = HEADS // KV_HEADS
    kv_local = key_cache.shape[2] // HEAD_DIM
    span_local = key_cache.shape[1]
    query_heads = queries.reshape(seq_count, kv_local, group_size, HEAD_DIM)
    key_rows = key_cache.reshape(seq_count, span_local, kv_local, HEAD_DIM)
    value_rows = value_cache.reshape(seq_count, span_local, kv_local, HEAD_DIM).astype(jnp.float32)
    first_place = lax.axis_index(SEQ) * span_local
    places = first_place + jnp.arange(span_local, dtype=jnp.int32)
    live_mask = (places[None, :] < lengths[:, None])[:, None, None, :]
    scores = jnp.einsum(
        "bkgd,bjkd->bkgj", query_heads, key_rows, preferred_element_type=jnp.float32
    ) * (1.0 / math.sqrt(HEAD_DIM))
    scores = jnp.where(live_mask, scores, masked_score)
    local_peak = jnp.max(scores, axis=-1)
    attn_weights = jnp.where(live_mask, jnp.exp(scores - local_peak[..., None]), 0.0)
    local_sum = jnp.einsum(
        "bkgj,bjkd->bkgd", attn_weights, value_rows, precision=lax.Precision.HIGHEST
    )
    global_peak, denom_sum, weighted = joined_all(
        (local_peak, jnp.sum(attn_weights, axis=-1), local_sum), SEQ, merge_partial_results
    )
    attended = (
        (weighted / denom_sum[..., None])
        .reshape(seq_count, kv_local * group_size * HEAD_DIM)
        .astype(jnp.bfloat16)
    )
    partial_value = jnp.dot(attended, out_weight, preferred_element_type=jnp.float32)
    projected = sent_and_summed(partial_value, "exp", 0)
    residual = hidden_in.astype(jnp.float32) + projected
    gained = residual * norm_gain
    router_wide = router.astype(jnp.float32)
    squares = jnp.sum(residual * residual, axis=-1)
    total_sq, raw_logits = packed_total(
        (squares, jnp.dot(gained, router_wide, precision=lax.Precision.HIGHEST)), SEQ
    )
    scale_row = lax.rsqrt(total_sq / D + norm_eps)
    logits = raw_logits * scale_row[:, None]
    normed = (gained * scale_row[:, None]).astype(jnp.bfloat16)
    row_total = expert_ids.shape[0]
    onehot_int = (
        expert_ids[:, :, None] == jnp.arange(EXPERTS, dtype=jnp.int32)[None, None, :]
    ).astype(jnp.int32)
    name_count = jnp.sum(onehot_int, axis=1)
    row_order = jnp.arange(row_total, dtype=jnp.int32)
    before = (row_order[None, :] < row_order[:, None]).astype(jnp.int32)
    earlier = jnp.dot(before, name_count)
    slot_rank = jnp.sum(onehot_int * earlier[:, None, :], axis=-1)
    slot_limit = jnp.sum(onehot_int * capacity[None, None, :], axis=-1)
    kept_mask = (slot_rank < slot_limit).astype(jnp.float32)
    expert_indicator = onehot_int.astype(jnp.float32)
    chosen = jnp.sum(expert_indicator * logits[:, None, :], axis=-1)
    gate_weight = jax.nn.sigmoid(chosen - chosen[:, ::-1])
    slot_match = (slot_rank[:, :, None] == row_order[None, None, :]).astype(jnp.float32)
    placing = jnp.einsum("rke,rks->esr", expert_indicator * kept_mask[:, :, None], slot_match)
    buffer = jnp.einsum(
        "esr,rd->esd", placing.astype(jnp.bfloat16), normed, preferred_element_type=jnp.float32
    ).astype(jnp.bfloat16)
    dispatched = lax.all_to_all(buffer, "exp", split_axis=0, concat_axis=1, tiled=True)
    shard_rows = gathered_copies(dispatched, SEQ, 2)
    gate_next = jnp.einsum("ern,enf->erf", shard_rows, w_gate, preferred_element_type=jnp.float32)
    up_next = jnp.einsum("ern,enf->erf", shard_rows, w_up, preferred_element_type=jnp.float32)
    hidden_act = (jax.nn.silu(gate_next) * up_next).astype(jnp.bfloat16)
    partial_out = jnp.einsum("erf,efd->erd", hidden_act, w_down, preferred_element_type=jnp.float32)
    blend_table = jnp.einsum(
        "rke,rks->esr", expert_indicator * (gate_weight * kept_mask)[:, :, None], slot_match
    )
    reduced_output = sent_and_summed(partial_out, SEQ, 2)
    returned = lax.all_to_all(reduced_output, "exp", split_axis=1, concat_axis=0, tiled=True)
    combined = jnp.einsum("esr,esd->rd", blend_table, returned, precision=lax.Precision.HIGHEST)
    return (residual + combined).astype(jnp.bfloat16)


def solution(mesh):
    split = Mesh(
        mesh.devices.reshape(4, 4, 2, mesh.shape["exp"]), ("seq_0", "seq_1", "seq_2", "exp")
    )
    placed = (
        P("exp", SEQ),
        P(None, "exp"),
        P(None, SEQ, "exp"),
        P(None, SEQ, "exp"),
        P(),
        P("exp", SEQ),
        P(SEQ),
        P(SEQ, None),
        P("exp", None),
        P(),
        P("exp", None, SEQ),
        P("exp", None, SEQ),
        P("exp", SEQ, None),
    )
    return jax.shard_map(
        on_device, mesh=split, in_specs=placed, out_specs=P("exp", SEQ), check_vma=False
    )
```

profile of v0, /device:TPU:32, one launch (start us, length us, event | category | flops | bytes accessed | tf_op | source)
XLA Modules:
  0.0 162.0 jit_solution(17786532491789367898)
XLA Ops:
  0.0 1.0 reshape.831
  1.0 0.7 broadcast_compare_fusion
  1.7 2.0 %fusion.88 = (f32[24,6]{1,0:T(8,128)S(1)}, f32[24,6,256]{2,1,0:T(8,128)S(1)}) fusion(bf16[24,6,128]{2,1,0:T(8,128)(2,1)S(1)} %reshape.831, bf16[24,256,128]{2,1,0:T(8,128)(2,1)} %param.15, pred[24,256]{1,0:T(8,128)(4,1)S(1)} %broadcast_compare_fusion), kind=kOutput, calls=%fused_computation.149 | convolution fusion | flops 9547632 | bytes 1763904 | tf_op jit(solution)/shard_map/bkgd,bjkd->bkgj/dot_general | solution.py:125
  4.0 2.2 %fusion.22 = f32[24,6,128]{2,1,0:T(8,128)S(1)} fusion(bf16[24,256,128]{2,1,0:T(8,128)(2,1)} %param.16, f32[24,6,256]{2,1,0:T(8,128)S(1)} %get-tuple-element.61, f32[24,6]{1,0:T(8,128)S(1)} %get-tuple-element.60, pred[24,256]{1,0:T(8,128)(4,1)S(1)} %broadcast_compare_fusion), kind=kOutput, calls=%fused_computation.21 | convolution fusion | flops 56696832 | bytes 1800768 | tf_op jit(solution)/shard_map/bkgj,bjkd->bkgd/dot_general | solution.py:131
  6.4 12.9 %all-gather.3 = f32[4,148,128]{2,1,0:T(8,128)S(1)} all-gather(f32[1,148,128]{2,1,0:T(8,128)S(1)} %maximum_bitcast_fusion), channel_id=2, replica_groups=mesh['seq_0'=4,'seq_1'=4,'seq_2'=2,'exp'=8] {'seq_0'}, dimensions={0}, use_global_device_ids=true | all-gather | bytes 378880 | tf_op jit(solution)/shard_map/all_gather | solution.py:29
  19.6 15.0 %all-gather.4 = f32[4,148,128]{2,1,0:T(8,128)S(1)} all-gather(f32[1,148,128]{2,1,0:T(8,128)S(1)} %maximum_bitcast_fusion.1), channel_id=3, replica_groups=mesh['seq_0'=4,'seq_1'=4,'seq_2'=2,'exp'=8] {'seq_1'}, dimensions={0}, use_global_device_ids=true | all-gather | bytes 378880 | tf_op jit(solution)/shard_map/all_gather | solution.py:29
  34.9 1.9 %all-gather.5 = f32[2,148,128]{2,1,0:T(8,128)S(1)} all-gather(f32[1,148,128]{2,1,0:T(8,128)S(1)} %maximum_bitcast_fusion.2), channel_id=4, replica_groups=mesh['seq_0'=4,'seq_1'=4,'seq_2'=2,'exp'=8] {'seq_2'}, dimensions={0}, use_global_device_ids=true | all-gather | bytes 227328 | tf_op jit(solution)/shard_map/all_gather | solution.py:29
  37.9 0.7 squeeze.114
  38.9 0.9 squeeze.117
  39.9 1.0 fusion.26
  40.8 1.1 fusion.19
  42.6 8.4 %all-to-all-start = ((f32[8,3,192]{2,1,0:T(4,128)}), f32[8,3,192]{2,1,0:T(4,128)S(1)}, u32[]{:S(2)}, u32[]{:S(2)}) async-start(f32[8,3,192]{2,1,0:T(4,128)} %copy.53), calls=%async_computation | async-start | bytes 65536 | tf_op jit(solution)/shard_map/all_to_all | solution.py:54
  51.4 9.8 %all-to-all-done = f32[8,3,192]{2,1,0:T(4,128)S(1)} async-done(((f32[8,3,192]{2,1,0:T(4,128)}), f32[8,3,192]{2,1,0:T(4,128)S(1)}, u32[]{:S(2)}, u32[]{:S(2)}) %all-to-all-start) | async-done | bytes 18464 | tf_op jit(solution)/shard_map/all_to_all | solution.py:54
  61.4 0.8 fusion.59
  63.0 7.2 %all-to-all-start.1 = ((f32[32,1,27]{2,1,0:T(1,128)}), f32[32,1,27]{2,1,0:T(1,128)S(1)}, u32[]{:S(2)}, u32[]{:S(2)}) async-start(f32[32,1,27]{2,1,0:T(1,128)} %broadcast_in_dim.27), calls=%async_computation.1 | async-start | bytes 32768 | tf_op jit(solution)/shard_map/all_to_all | solution.py:60
  70.2 0.9 select_reduce_fusion
  71.1 5.5 %all-to-all-done.1 = f32[32,1,27]{2,1,0:T(1,128)S(1)} async-done(((f32[32,1,27]{2,1,0:T(1,128)}), f32[32,1,27]{2,1,0:T(1,128)S(1)}, u32[]{:S(2)}, u32[]{:S(2)}) %all-to-all-start.1) | async-done | bytes 3488 | tf_op jit(solution)/shard_map/all_to_all | solution.py:60
  78.1 0.9 convolution_convert_fusion
  79.0 12.5 %all_to_all.42 = bf16[8,3,192]{2,1,0:T(4,128)(2,1)S(1)} all-to-all(bf16[8,3,192]{2,1,0:T(4,128)(2,1)S(1)} %copy.57), channel_id=1, replica_groups=mesh['seq_0'=4,'seq_1'=4,'seq_2'=2,'exp'=8] {'exp'}, dimensions={0} | all-to-all | bytes 18432 | tf_op jit(solution)/shard_map/all_to_all | solution.py:173
  91.5 0.8 broadcast_in_dim.29
  92.3 5.0 %all-to-all-start.3 = ((bf16[32,1,24,192]{3,2,1,0:T(8,128)(2,1)}), bf16[32,1,24,192]{3,2,1,0:T(8,128)(2,1)S(1)}, u32[]{:S(2)}, u32[]{:S(2)}) async-start(bf16[32,1,24,192]{3,2,1,0:T(8,128)(2,1)} %broadcast_in_dim.29), calls=%async_computation.3 | async-start | bytes 786432 | tf_op jit(solution)/shard_map/all_to_all | solution.py:60
  97.3 4.6 %copy.59 = bf16[1,256,6144]{1,2,0:T(8,128)(2,1)} copy(bf16[1,256,6144]{2,1,0:T(8,128)(2,1)} %param.25) | data formatting | bytes 6291456 | tf_op args[12]
  101.9 7.9 %all-to-all-done.3 = bf16[32,1,24,192]{3,2,1,0:T(8,128)(2,1)S(1)} async-done(((bf16[32,1,24,192]{3,2,1,0:T(8,128)(2,1)}), bf16[32,1,24,192]{3,2,1,0:T(8,128)(2,1)S(1)}, u32[]{:S(2)}, u32[]{:S(2)}) %all-to-all-start.3) | async-done | bytes 294944 | tf_op jit(solution)/shard_map/all_to_all | solution.py:60
  109.8 0.8 copy.58
  110.6 1.5 reshape.849
  112.1 2.4 %fusion.2 = f32[24,256]{1,0:T(8,128)S(1)} fusion(bf16[24,6144]{1,0:T(8,128)(2,1)S(1)} %reshape.849, bf16[1,6144,256]{2,1,0:T(8,128)(2,1)} %param.23), kind=kOutput, calls=%fused_computation.2 | convolution fusion | flops 75497472 | bytes 3465216 | tf_op jit(solution)/shard_map/ern,enf->erf/dot_general | solution.py:175
  114.5 5.0 %convolution_bitcast_fusion = f32[32,1,24,192]{3,2,1,0:T(8,128)} fusion(bf16[32,192,256]{2,1,0:T(8,128)(2,1)} %bitcast.184, bf16[24,6144]{1,0:T(8,128)(2,1)S(1)} %reshape.849, bf16[1,6144,256]{2,1,0:T(8,128)(2,1)S(1)} %copy-done, f32[24,256]{1,0:T(8,128)S(1)} %fusion.2), kind=kOutput, calls=%fused_computation.4 | convolution fusion | flops 151031808 | bytes 7200768 | tf_op jit(solution)/shard_map/erf,efd->erd/dot_general | solution.py:178
  119.5 26.4 %all_to_all.43 = f32[32,1,24,192]{3,2,1,0:T(8,128)} all-to-all(f32[32,1,24,192]{3,2,1,0:T(8,128)} %convolution_bitcast_fusion), channel_id=1, replica_groups=mesh['seq_0'=4,'seq_1'=4,'seq_2'=2,'exp'=8] {'seq_0','seq_1','seq_2'}, dimensions={0} | all-to-all | bytes 1179648 | tf_op jit(solution)/shard_map/all_to_all | solution.py:54
  145.9 1.2 reduce_sum.91
  147.7 3.3 %all-to-all-start.5 = ((f32[1,24,192]{2,0,1:T(1,128)}), f32[1,24,192]{2,0,1:T(1,128)S(1)}, u32[]{:S(2)}, u32[]{:S(2)}) async-start(f32[1,24,192]{2,0,1:T(1,128)} %reduce_sum.92), calls=%async_computation.5 | async-start | bytes 49152 | tf_op jit(solution)/shard_map/all_to_all | solution.py:183
  151.3 9.8 %all-to-all-done.5 = f32[1,24,192]{2,0,1:T(1,128)S(1)} async-done(((f32[1,24,192]{2,0,1:T(1,128)}), f32[1,24,192]{2,0,1:T(1,128)S(1)}, u32[]{:S(2)}, u32[]{:S(2)}) %all-to-all-start.5) | async-done | bytes 18464 | tf_op jit(solution)/shard_map/all_to_all | solution.py:183
  161.2 0.8 fusion.16
  (81 shorter events, 6.7 us)
Async XLA Ops:
  0.0 114.5 %copy-start = (bf16[1,6144,256]{2,1,0:T(8,128)(2,1)S(1)}, bf16[1,6144,256]{2,1,0:T(8,128)(2,1)}, u32[]{:S(2)}) copy-start(bf16[1,6144,256]{2,1,0:T(8,128)(2,1)} %param.24) | copy-start | bytes 9437188
  6.2 44.8 %copy-start.3 = (s32[3,2]{0,1:T(2,128)S(1)}, s32[3,2]{0,1:T(2,128)}, u32[]{:S(2)}) copy-start(s32[3,2]{0,1:T(2,128)} %param.21) | copy-start | bytes 76
  6.2 55.0 %copy-start.1 = (bf16[3,192]{1,0:T(4,128)(2,1)S(1)}, bf16[3,192]{1,0:T(4,128)(2,1)}, u32[]{:S(2)}) copy-start(bf16[3,192]{1,0:T(4,128)(2,1)} %param.13) | copy-start | bytes 3460
  6.2 55.1 %copy-start.4 = (bf16[192,8]{0,1:T(8,128)(2,1)S(1)}, bf16[192,8]{0,1:T(8,128)(2,1)}, u32[]{:S(2)}) copy-start(bf16[192,8]{0,1:T(8,128)(2,1)} %param.20) | copy-start | bytes 9220
  42.6 18.6 %all-to-all-start = ((f32[8,3,192]{2,1,0:T(4,128)}), f32[8,3,192]{2,1,0:T(4,128)S(1)}, u32[]{:S(2)}, u32[]{:S(2)}) async-start(f32[8,3,192]{2,1,0:T(4,128)} %copy.53), calls=%async_computation | async-start | bytes 65536 | tf_op jit(solution)/shard_map/all_to_all | solution.py:54
  63.0 13.7 %all-to-all-start.1 = ((f32[32,1,27]{2,1,0:T(1,128)}), f32[32,1,27]{2,1,0:T(1,128)S(1)}, u32[]{:S(2)}, u32[]{:S(2)}) async-start(f32[32,1,27]{2,1,0:T(1,128)} %broadcast_in_dim.27), calls=%async_computation.1 | async-start | bytes 32768 | tf_op jit(solution)/shard_map/all_to_all | solution.py:60
  92.3 17.5 %all-to-all-start.3 = ((bf16[32,1,24,192]{3,2,1,0:T(8,128)(2,1)}), bf16[32,1,24,192]{3,2,1,0:T(8,128)(2,1)S(1)}, u32[]{:S(2)}, u32[]{:S(2)}) async-start(bf16[32,1,24,192]{3,2,1,0:T(8,128)(2,1)} %broadcast_in_dim.29), calls=%async_computation.3 | async-start | bytes 786432 | tf_op jit(solution)/shard_map/all_to_all | solution.py:60
  114.5 36.6 %copy-start.2 = (f32[3,2]{1,0:T(4,128)S(1)}, f32[3,2]{1,0:T(4,128)}, u32[]{:S(2)}) copy-start(f32[3,2]{1,0:T(4,128)} %get-tuple-element.11) | copy-start | bytes 76
  147.7 13.4 %all-to-all-start.5 = ((f32[1,24,192]{2,0,1:T(1,128)}), f32[1,24,192]{2,0,1:T(1,128)S(1)}, u32[]{:S(2)}, u32[]{:S(2)}) async-start(f32[1,24,192]{2,0,1:T(1,128)} %reduce_sum.92), calls=%async_computation.5 | async-start | bytes 49152 | tf_op jit(solution)/shard_map/all_to_all | solution.py:183
where the time goes:
time: 165 us; the launch traced here: 162 us
  blocking collectives  68.7 us (42%)
  waiting for transfers between devices  33.1 us (20%)
  starting transfers between devices  24 us (15%)
  matrix products  15.8 us (10%)
  local copies, waits for them, and re-layouts  14.3 us (9%)
  other arithmetic  5.71 us (3%)
    all_gather x3, blocking collectives, collected_together(): both, at, found = (lax.all_gather(jnp.concatenate(lines), axis), 0, {})  29.8 us
    all_to_all x1, blocking collectives, sent_and_summed(): lax.all_to_all(pieces, axis, split_axis=0, concat_axis=0, tiled=True)  26.4 us
    all_to_all x2, waiting for transfers between devices, copy_for_each(): lax.all_to_all(jnp.broadcast_to(value[None], (devices, *value.shape)), ax...  13.4 us
    all_to_all x1, blocking collectives, on_device(): lax.all_to_all(buffer, 'exp', split_axis=0, concat_axis=1, tiled=True)  12.5 us
    all_to_all x2, starting transfers between devices, copy_for_each(): lax.all_to_all(jnp.broadcast_to(value[None], (devices, *value.shape)), ax...  12.2 us
    all_to_all x1, waiting for transfers between devices, sent_and_summed(): lax.all_to_all(pieces, axis, split_axis=0, concat_axis=0, tiled=True)  9.85 us
    all_to_all x1, waiting for transfers between devices, on_device(): lax.all_to_all(reduced_output, 'exp', split_axis=1, concat_axis=0, tiled=...  9.81 us
    all_to_all x1, starting transfers between devices, sent_and_summed(): lax.all_to_all(pieces, axis, split_axis=0, concat_axis=0, tiled=True)  8.45 us
  transfers between devices with their start and end apart: 4, of which 4 were waited for; matrix products, arithmetic and copies ran while one was open for 4% of the time, Pallas kernels for 0%

commit v1 on v0

v1 whole, which is shorter than its diff:
```python
import functools
import math

import jax
import jax.numpy as jnp
from jax import lax
from jax.experimental import pallas as pl
from jax.experimental.pallas import tpu as pltpu
from jax.sharding import Mesh
from jax.sharding import PartitionSpec as P

D = 6144
HEADS = 48
KV_HEADS = 8
HEAD_DIM = 128
EXPERTS = 8
TOKENS = 24
OWNED = 3
GROUP = HEADS // KV_HEADS
COLS = 192
HALF = TOKENS // 2
SUB = 8
HALF_ROWS = HALF * SUB
CHIPS = 16
SEQ = ("seq_0", "seq_1", "seq_2")
masked_score = -1e30
norm_eps = 1e-05
f32 = jnp.float32
bf16 = jnp.bfloat16
VMEM = pl.BlockSpec(memory_space=pltpu.VMEM)
SMEM = pl.BlockSpec(memory_space=pltpu.SMEM)
ANY = pl.BlockSpec(memory_space=pl.ANY)


def lanes(shape):
    return lax.broadcasted_iota(jnp.int32, shape, len(shape) - 1)


def subs(shape):
    return lax.broadcasted_iota(jnp.int32, shape, len(shape) - 2)


def rounded(x):
    return x.astype(bf16).astype(f32)


CHUNKS = 4
PER = TOKENS // CHUNKS


def attention_kernel(where_ref, lengths_ref, q_ref, k_any, v_any, out_ref, kbuf, vbuf, qs, sems):
    copies = []
    for i in range(CHUNKS):
        part = pl.ds(i * PER, PER)
        copies.append(
            (
                pltpu.make_async_copy(k_any.at[part], kbuf.at[part], sems.at[0, i]),
                pltpu.make_async_copy(v_any.at[part], vbuf.at[part], sems.at[1, i]),
            )
        )
    for pair in copies:
        pair[0].start()
        pair[1].start()
    qs[...] = jnp.zeros_like(qs)
    for h in range(GROUP):
        qs[pl.ds(h, TOKENS, stride=SUB), :] = q_ref[:, h * HEAD_DIM : (h + 1) * HEAD_DIM].astype(f32)
    first = where_ref[0]
    span = k_any.shape[1]
    places = first + lanes((SUB, span))
    lane, sub = lanes((SUB, 128)), subs((SUB, 128))
    scale = 1.0 / math.sqrt(HEAD_DIM)
    for i in range(CHUNKS):
        copies[i][0].wait()
        scores = []
        for b in range(i * PER, (i + 1) * PER):
            query = qs[b * SUB : (b + 1) * SUB, :].astype(bf16)
            s = lax.dot_general(query, kbuf[b], (((1,), (1,)), ((), ())), preferred_element_type=f32)
            scores.append(jnp.where(places < lengths_ref[b], s * scale, masked_score))
        copies[i][1].wait()
        blocks = []
        for n, b in enumerate(range(i * PER, (i + 1) * PER)):
            s = scores[n]
            peak = rounded(jnp.max(s, axis=-1, keepdims=True))
            p = jnp.where(places < lengths_ref[b], jnp.exp(s - peak), 0.0)
            total = jnp.sum(p, axis=-1, keepdims=True)
            p_hi = rounded(p)
            both = jnp.concatenate([p_hi, p - p_hi], axis=0).astype(bf16)
            weighted = jnp.dot(both, vbuf[b], preferred_element_type=f32)
            weighted = weighted[:SUB] + weighted[SUB:]
            total_hi = rounded(total)
            stats = jnp.where(lane == sub, peak, 0.0)
            stats = jnp.where(lane == sub + SUB, total_hi, stats)
            stats = jnp.where(lane == sub + 2 * SUB, total - total_hi, stats)
            stats = jnp.sum(jnp.where(sub < GROUP, stats, 0.0), axis=0, keepdims=True)
            blocks.append(jnp.where(sub == GROUP, stats, weighted))
        for n in range(0, PER, 2):
            b = i * PER + n
            half, row = b // HALF, (b % HALF) * SUB
            two = jnp.concatenate([blocks[n], blocks[n + 1]], axis=0).astype(bf16)
            for y in range(4):
                out_ref[2 * y + half, row : row + 2 * SUB, :] = two


def combined(blocks):
    shape = (HALF, SUB, 128)
    lane, sub = lanes(shape), subs(shape)
    flat = lanes((HALF, 1, 128))
    stats = [jnp.sum(jnp.where(sub == GROUP, x, 0.0), axis=1, keepdims=True) for x in blocks]
    peak = functools.reduce(jnp.maximum, stats)
    factors = [jnp.exp(jnp.minimum(s - peak, 0.0)) for s in stats]
    total = jnp.zeros((HALF, 1, 128), f32)
    for s, factor in zip(stats, factors):
        total += factor * (pltpu.roll(s, 128 - SUB, 2) + pltpu.roll(s, 128 - 2 * SUB, 2))
    total = jnp.where(flat < GROUP, total, 1.0)
    return peak, factors, total


def as_column(x):
    shape = (HALF, SUB, 128)
    wide = jnp.broadcast_to(x, shape)
    return jnp.sum(jnp.where(lanes(shape) == subs(shape), wide, 0.0), axis=2, keepdims=True)


def merge_kernel(in_ref, out_ref):
    blocks = [in_ref[i].astype(f32).reshape(HALF, SUB, 128) for i in range(8)]
    peak, factors, total = combined(blocks)
    weighted = jnp.zeros((HALF, SUB, 128), f32)
    for x, factor in zip(blocks, factors):
        weighted += as_column(factor) * x
    flat = lanes((HALF, 1, 128))
    total_hi = rounded(total)
    stats = jnp.where(flat < SUB, peak, pltpu.roll(total_hi, SUB, 2))
    stats = jnp.where(flat < 2 * SUB, stats, pltpu.roll(total - total_hi, 2 * SUB, 2))
    stats = jnp.where(flat < 3 * SUB, stats, 0.0)
    sub = subs((HALF, SUB, 128))
    block = jnp.where(sub == GROUP, stats, weighted).reshape(HALF_ROWS, 128).astype(bf16)
    for i in range(8):
        out_ref[i] = block


def project_kernel(where_ref, ids_ref, in_ref, hidden_ref, weight_ref, out_ref, rest_ref, att, wide):
    for half in range(2):
        blocks = [in_ref[2 * z + half].astype(f32).reshape(HALF, SUB, 128) for z in range(4)]
        _, factors, total = combined(blocks)
        inverse = 1.0 / total
        weighted = jnp.zeros((HALF, SUB, 128), f32)
        for x, factor in zip(blocks, factors):
            weighted += as_column(factor * inverse) * x
        att[half * HALF_ROWS : (half + 1) * HALF_ROWS, :] = weighted.reshape(HALF_ROWS, 128)
    acc = jnp.zeros((TOKENS, COLS), f32)
    for h in range(GROUP):
        rows = att[pl.ds(h, TOKENS, stride=SUB), :].astype(bf16)
        acc += lax.dot_general(
            rows,
            weight_ref[:, h * HEAD_DIM : (h + 1) * HEAD_DIM],
            (((1,), (1,)), ((), ())),
            preferred_element_type=f32,
        )
    mine = OWNED * where_ref[1]
    row = subs((TOKENS, COLS))
    hidden = hidden_ref[...].astype(f32)
    for r in range(OWNED):
        acc += jnp.where(row == mine + r, hidden[r : r + 1, :], 0.0)
    tail = jnp.zeros((TOKENS, 64), f32)
    lane, row_tail = lanes((TOKENS, 64)), subs((TOKENS, 64))
    for r in range(OWNED):
        for k in range(2):
            here = (row_tail == mine + r) & (lane == k)
            tail = jnp.where(here, ids_ref[k, r].astype(f32), tail)
    wide[:, :COLS] = acc
    wide[:, COLS:] = tail
    full = wide[...]
    sent = full.astype(bf16)
    for i in range(8):
        out_ref[i] = sent
    row = subs((TOKENS, 256))
    owned = (row >= mine) & (row < mine + OWNED)
    rest_ref[...] = jnp.where(owned, full - sent.astype(f32), 0.0)


def gained_kernel(in_ref, rest_ref, gain_ref, router_ref, out_ref, residual_ref, wide):
    total = rest_ref[...]
    for i in range(8):
        total += in_ref[i].astype(f32)
    residual_ref[...] = total
    residual = total[:, :COLS]
    gained = residual * gain_ref[...]
    hi = gained.astype(bf16)
    lo = (gained - hi.astype(f32)).astype(bf16)
    over_features = (((1,), (1,)), ((), ()))
    logits = lax.dot_general(hi, router_ref[...], over_features, preferred_element_type=f32)
    logits += lax.dot_general(lo, router_ref[...], over_features, preferred_element_type=f32)
    squares = jnp.sum(residual * residual, axis=-1, keepdims=True)
    logits_hi, squares_hi = rounded(logits), rounded(squares)
    wide[...] = jnp.zeros_like(wide)
    wide[:, :COLS] = gained
    wide[:, COLS : COLS + 8] = logits_hi
    wide[:, COLS + 8 : COLS + 9] = squares_hi
    wide[:, COLS + 32 : COLS + 40] = logits - logits_hi
    wide[:, COLS + 40 : COLS + 41] = squares - squares_hi
    sent = wide[...].astype(bf16)
    for i in range(CHIPS):
        out_ref[i] = sent


def expert_kernel(
    where_ref, capacity_ref, own_ref, other_ref, residual_ref, gate_ref, up_ref, down_ref, keep_ref, send_ref
):
    core, me = where_ref[2], where_ref[1]
    stats = jnp.zeros((TOKENS, 128), f32)
    gate = jnp.zeros((TOKENS, 256), f32)
    up = jnp.zeros((TOKENS, 256), f32)
    for k in range(CHIPS):
        for ref, parity in ((own_ref, core), (other_ref, 1 - core)):
            stats += ref[k, :, 128:].astype(f32)
            rows = pl.ds(pl.multiple_of((2 * k + parity) * COLS, COLS), COLS)
            x = ref[k, :, :COLS]
            gate += jnp.dot(x, gate_ref[rows, :], preferred_element_type=f32)
            up += jnp.dot(x, up_ref[rows, :], preferred_element_type=f32)
    stats = pltpu.roll(stats, 64, 1) + pltpu.roll(stats, 32, 1)
    lane, row = lanes((TOKENS, 128)), subs((TOKENS, 128))

    def pick(x, place):
        return jnp.sum(jnp.where(lane == place, x, 0.0), axis=-1, keepdims=True)

    scale = lax.rsqrt(pick(stats, 8) / D + norm_eps)
    logits = stats * scale
    named = residual_ref[:, 128:]
    first, second = pick(named, 64).astype(jnp.int32), pick(named, 65).astype(jnp.int32)
    names = (first == me) | (second == me)
    other = jnp.where(first == me, second, first)
    routed = 1.0 / (1.0 + jnp.exp(pick(logits, other) - pick(logits, me)))
    naming = jnp.broadcast_to(jnp.where(names, 1.0, 0.0), (TOKENS, 128))
    place = row % OWNED
    earlier = jnp.where(place >= 1, pltpu.roll(naming, 1, 0), 0.0)
    earlier += jnp.where(place >= 2, pltpu.roll(naming, 2, 0), 0.0)
    earlier = earlier[:, :1]
    kept = names & (earlier < capacity_ref[me].astype(f32))
    weight = jnp.where(kept, routed, 0.0)
    gate, up = gate * scale, up * scale
    inner = (gate / (1.0 + jnp.exp(-gate)) * up * weight).astype(bf16)
    for k in range(CHIPS):
        y = jnp.dot(inner, down_ref[:, 2 * COLS * k : 2 * COLS * (k + 1)], preferred_element_type=f32)
        even, odd = y[:, :COLS], y[:, COLS:]
        keep_ref[k] = jnp.where(core == 0, even, odd)
        send_ref[k] = jnp.where(core == 0, odd, even).astype(bf16)


def pair_kernel(keep_ref, got_ref, out_ref):
    for k in range(CHIPS):
        total = (keep_ref[k] + got_ref[k].astype(f32)).astype(bf16).astype(f32)
        for e in range(EXPERTS):
            out_ref[EXPERTS * k + e] = total[OWNED * e : OWNED * (e + 1), :].astype(bf16)


def final_kernel(where_ref, in_ref, residual_ref, out_ref):
    me = where_ref[1]
    total = jnp.zeros((OWNED, COLS), f32)
    for e in range(EXPERTS):
        rows = residual_ref[OWNED * e : OWNED * (e + 1), :COLS]
        total += jnp.where(me == e, rows, 0.0)
    out_ref[...] = (total + jnp.sum(in_ref[...].astype(f32), axis=0)).astype(bf16)


def shaped(shape, dtype):
    return jax.ShapeDtypeStruct(shape, dtype)


def call(kernel, outs, specs, scratch=(), limit=None):
    single = not isinstance(outs, tuple)
    return pl.pallas_call(
        kernel,
        out_shape=outs,
        in_specs=list(specs),
        out_specs=VMEM if single else (VMEM,) * len(outs),
        scratch_shapes=list(scratch),
        compiler_params=pltpu.CompilerParams(vmem_limit_bytes=limit),
    )


def exchanged(value, axes):
    return lax.all_to_all(value, axes, 0, 0, tiled=True)


def swapped(value):
    return lax.ppermute(value, "seq_2", [(0, 1), (1, 0)])


def on_device(
    hidden_in,
    queries,
    key_cache,
    value_cache,
    lengths,
    out_weight,
    norm_gain,
    router,
    expert_ids,
    capacity,
    w_gate,
    w_up,
    w_down,
):
    span = key_cache.shape[1]
    where = jnp.stack(
        [lax.axis_index(SEQ) * span, lax.axis_index("exp"), lax.axis_index("seq_2")]
    ).astype(jnp.int32)
    partial = call(
        attention_kernel,
        shaped((8, HALF_ROWS, 128), bf16),
        (SMEM, SMEM, VMEM, ANY, ANY),
        (
            pltpu.VMEM(key_cache.shape, bf16),
            pltpu.VMEM(value_cache.shape, bf16),
            pltpu.VMEM((TOKENS * SUB, 128), f32),
            pltpu.SemaphoreType.DMA((2, CHUNKS)),
        ),
        limit=12 << 20,
    )(where, lengths, queries, key_cache, value_cache)
    partial = exchanged(partial, ("seq_0", "seq_2"))
    partial = call(merge_kernel, shaped((8, HALF_ROWS, 128), bf16), (VMEM,))(partial)
    partial = exchanged(partial, ("seq_1", "seq_2"))
    projected, rest = call(
        project_kernel,
        (shaped((8, TOKENS, 256), bf16), shaped((TOKENS, 256), f32)),
        (SMEM, SMEM, VMEM, VMEM, VMEM),
        (pltpu.VMEM((TOKENS * SUB, 128), f32), pltpu.VMEM((TOKENS, 256), f32)),
    )(where, expert_ids.T, partial, hidden_in, out_weight.T)
    projected = exchanged(projected, "exp")
    gained, residual = call(
        gained_kernel,
        (shaped((CHIPS, TOKENS, 256), bf16), shaped((TOKENS, 256), f32)),
        (VMEM,) * 4,
        (pltpu.VMEM((TOKENS, 256), f32),),
    )(projected, rest, norm_gain[None, :], router.T)
    own = exchanged(gained, ("seq_0", "seq_1"))
    other = swapped(own)
    keep, send = call(
        expert_kernel,
        (shaped((CHIPS, TOKENS, COLS), f32), shaped((CHIPS, TOKENS, COLS), bf16)),
        (SMEM, SMEM) + (VMEM,) * 6,
        limit=24 << 20,
    )(where, capacity, own, other, residual, w_gate[0], w_up[0], w_down[0])
    got = swapped(send)
    summed = call(pair_kernel, shaped((CHIPS * EXPERTS, OWNED, COLS), bf16), (VMEM, VMEM))(keep, got)
    summed = exchanged(summed, ("seq_0", "seq_1", "exp"))
    return call(final_kernel, shaped((OWNED, COLS), bf16), (SMEM, VMEM, VMEM))(where, summed, residual)


def solution(mesh):
    split = Mesh(
        mesh.devices.reshape(4, 4, 2, mesh.shape["exp"]), ("seq_0", "seq_1", "seq_2", "exp")
    )
    placed = (
        P("exp", SEQ),
        P(None, "exp"),
        P(None, SEQ, "exp"),
        P(None, SEQ, "exp"),
        P(),
        P("exp", SEQ),
        P(SEQ),
        P(SEQ, None),
        P("exp", None),
        P(),
        P("exp", None, SEQ),
        P("exp", None, SEQ),
        P("exp", SEQ, None),
    )
    return jax.shard_map(
        on_device, mesh=split, in_specs=placed, out_specs=P("exp", SEQ), check_vma=False
    )
```

time: 165 us -> 109 us (0.66); the launches traced: 162 us -> 108 us
  waiting for transfers between devices: 33.1 us -> 2.74 us
  starting transfers between devices: 24 us -> 0.14 us
  Pallas kernels: 0 us -> 16.4 us
  matrix products: 15.8 us -> 0 us
  blocking collectives: 68.7 us -> 78.1 us
  other arithmetic: 5.71 us -> 0.08 us
  local copies, waits for them, and re-layouts: 14.3 us -> 11 us
    all_to_all x2 -> x5, blocking collectives: 38.9 us -> 78.1 us  [exchanged(): return lax.all_to_all(value, axes, 0, 0, tiled=True)]
    all_to_all x4 -> x0, waiting for transfers between devices: 33.1 us -> none  [the longest x2 13.4 us: copy_for_each(): lax.all_to_all(jnp.broadcast_to(value[None], (devices, *value.shape)), ax...]
    all_gather x3 -> x0, blocking collectives: 29.8 us -> none  [collected_together(): both, at, found = (lax.all_gather(jnp.concatenate(lines), axis), 0, {})]
    all_to_all x4 -> x0, starting transfers between devices: 24 us -> none  [the longest x2 12.2 us: copy_for_each(): lax.all_to_all(jnp.broadcast_to(value[None], (devices, *value.shape)), ax...]
    pallas_call x0 -> x7, Pallas kernels: none -> 16.4 us  [the longest x1 3.99 us: on_device(): call(attention_kernel, shaped((8, HALF_ROWS, 128), bf16), (SMEM, SMEM, VM...]
    dot_general x11 -> x0, matrix products: 15.8 us -> none  [the longest x1 5 us: on_device(): jnp.einsum('erf,efd->erd', hidden_act, w_down, preferred_element_type=jnp...]
    unnamed x21 -> x26, local copies, waits for them, and re-layouts: 4.8 us -> 11 us
    ppermute x0 -> x2, waiting for transfers between devices: none -> 2.74 us  [swapped(): return lax.ppermute(value, 'seq_2', [(0, 1), (1, 0)])]
  transfers between devices with their start and end apart: 4 -> 2, of which waited for: 4 -> 2; matrix products, arithmetic and copies ran while one was open for 4% -> 0% of each run, Pallas kernels for 0% -> 0%
where the time goes in v1:
time: 109 us; the launch traced here: 108 us
  blocking collectives  78.1 us (72%)
  Pallas kernels  16.4 us (15%)
  local copies, waits for them, and re-layouts  11 us (10%)
  waiting for transfers between devices  2.74 us (3%)
    all_to_all x5, blocking collectives, exchanged(): return lax.all_to_all(value, axes, 0, 0, tiled=True)  78.1 us
    unnamed x26, local copies, waits for them, and re-layouts  11 us
    pallas_call x1, Pallas kernels, on_device(): call(attention_kernel, shaped((8, HALF_ROWS, 128), bf16), (SMEM, SMEM, VM...  3.99 us
    ppermute x2, waiting for transfers between devices, swapped(): return lax.ppermute(value, 'seq_2', [(0, 1), (1, 0)])  2.74 us
    pallas_call x1, Pallas kernels, on_device(): call(expert_kernel, (shaped((CHIPS, TOKENS, COLS), f32), shaped((CHIPS, T...  2.53 us
    pallas_call x1, Pallas kernels, on_device(): call(project_kernel, (shaped((8, TOKENS, 256), bf16), shaped((TOKENS, 256...  2.38 us
  transfers between devices with their start and end apart: 2, of which 2 were waited for; matrix products, arithmetic and copies ran while one was open for 0% of the time, Pallas kernels for 0%

profile of v1, /device:TPU:32, one launch (start us, length us, event | category | flops | bytes accessed | tf_op | source)
XLA Modules:
  0.0 108.5 jit_solution(9152533888113845754)
XLA Ops:
  0.0 0.0 copy-start
  0.0 0.1 pad_add_fusion.where_ref
  0.1 1.6 %copy-done.3 = bf16[24,256,128]{2,1,0:T(8,128)(2,1)S(1)} copy-done((bf16[24,256,128]{2,1,0:T(8,128)(2,1)S(1)}, bf16[24,256,128]{2,1,0:T(8,128)(2,1)}, u32[]{:S(2)}) %copy-start.3) | copy-done | bytes 1572888
  1.6 1.4 %copy-done.4 = bf16[24,256,128]{2,1,0:T(8,128)(2,1)S(1)} copy-done((bf16[24,256,128]{2,1,0:T(8,128)(2,1)S(1)}, bf16[24,256,128]{2,1,0:T(8,128)(2,1)}, u32[]{:S(2)}) %copy-start.4) | copy-done | bytes 1572888
  3.0 0.8 copy-done.7
  3.8 0.7 copy-done.10
  4.5 4.0 %shard_map.127 = bf16[8,96,128]{2,1,0:T(8,128)(2,1)S(1)} custom-call(s32[3]{0:T(128)S(1)} %pad_add_fusion.where_ref, s32[24]{0:T(128)S(1)} %copy-done.10, bf16[24,768]{1,0:T(8,128)(2,1)S(1)} %copy-done.7, bf16[24,256,128]{2,1,0:T(8,128)(2,1)S(1)} %copy-done.3, bf16[24,256,128]{2,1,0:T(8,128)(2,1)S(1)} %copy-done.4), custom_call_target="tpu_custom_call" | custom-call | tf_op jit(solution)/shard_map/pallas_call | solution.py:308
  8.5 11.2 %all_to_all.25.in_ref = bf16[8,96,128]{2,1,0:T(8,128)(2,1)} all-to-all(bf16[8,96,128]{2,1,0:T(8,128)(2,1)S(1)} %shard_map.127), channel_id=1, replica_groups=mesh['seq_0'=4,'seq_1'=4,'seq_2'=2,'exp'=8] {'seq_0','seq_2'}, dimensions={0} | all-to-all | bytes 393216 | tf_op jit(solution)/shard_map/all_to_all | solution.py:282
  19.7 2.0 %shard_map.128 = bf16[8,96,128]{2,1,0:T(8,128)(2,1)} custom-call(bf16[8,96,128]{2,1,0:T(8,128)(2,1)} %all_to_all.25.in_ref), custom_call_target="tpu_custom_call" | custom-call | tf_op jit(solution)/shard_map/pallas_call | solution.py:321
  21.7 12.8 %all_to_all.26.in_ref = bf16[8,96,128]{2,1,0:T(8,128)(2,1)} all-to-all(bf16[8,96,128]{2,1,0:T(8,128)(2,1)} %shard_map.128), channel_id=1, replica_groups=mesh['seq_0'=4,'seq_1'=4,'seq_2'=2,'exp'=8] {'seq_1','seq_2'}, dimensions={0} | all-to-all | bytes 393216 | tf_op jit(solution)/shard_map/all_to_all | solution.py:282
  34.6 0.0 copy-done.8
  34.6 2.4 %shard_map.129 = (bf16[8,24,256]{2,1,0:T(8,128)(2,1)}, f32[24,256]{1,0:T(8,128)}) custom-call(s32[3]{0:T(128)} %copy-done.8, s32[2,3]{1,0:T(2,128)} %bitcast.15, bf16[8,96,128]{2,1,0:T(8,128)(2,1)} %all_to_all.26.in_ref, bf16[3,192]{1,0:T(4,128)(2,1)} %hidden_ref.1, bf16[192,768]{1,0:T(8,128)(2,1)} %bitcast.13), custom_call_target="tpu_custom_call" | custom-call | tf_op jit(solution)/shard_map/pallas_call | solution.py:323
  36.9 19.5 %all_to_all.27.in_ref = bf16[8,24,256]{2,1,0:T(8,128)(2,1)} all-to-all(bf16[8,24,256]{2,1,0:T(8,128)(2,1)} %get-tuple-element.11), channel_id=1, replica_groups=mesh['seq_0'=4,'seq_1'=4,'seq_2'=2,'exp'=8] {'exp'}, dimensions={0} | all-to-all | bytes 196608 | tf_op jit(solution)/shard_map/all_to_all | solution.py:282
  56.5 1.8 %shard_map.130 = (bf16[16,24,256]{2,1,0:T(8,128)(2,1)}, f32[24,256]{1,0:T(8,128)}) custom-call(bf16[8,24,256]{2,1,0:T(8,128)(2,1)} %all_to_all.27.in_ref, f32[24,256]{1,0:T(8,128)} %get-tuple-element.12.rest_ref, f32[1,192]{1,0:T(1,128)} %bitcast.16, bf16[8,192]{1,0:T(8,128)(2,1)} %bitcast.14), custom_call_target="tpu_custom_call" | custom-call | tf_op jit(solution)/shard_map/pallas_call | solution.py:330
  58.3 12.6 %all_to_all.28.own_ref = bf16[16,24,256]{2,1,0:T(8,128)(2,1)S(1)} all-to-all(bf16[16,24,256]{2,1,0:T(8,128)(2,1)} %get-tuple-element.13), channel_id=1, replica_groups=mesh['seq_0'=4,'seq_1'=4,'seq_2'=2,'exp'=8] {'seq_0','seq_1'}, dimensions={0} | all-to-all | bytes 393216 | tf_op jit(solution)/shard_map/all_to_all | solution.py:282
  70.9 0.0 collective-permute-start
  70.9 1.4 %collective-permute-done.other_ref = bf16[16,24,256]{2,1,0:T(8,128)(2,1)S(1)} collective-permute-done((bf16[16,24,256]{2,1,0:T(8,128)(2,1)S(1)}, bf16[16,24,256]{2,1,0:T(8,128)(2,1)S(1)}, u32[]{:S(2)}, u32[]{:S(2)}) %collective-permute-start) | collective-permute-done | bytes 196640 | tf_op jit(solution)/shard_map/ppermute | solution.py:286
  72.4 0.0 copy-done
  72.4 0.0 copy-done.11
  72.4 1.9 %copy-done.1 = bf16[1,6144,256]{2,1,0:T(8,128)(2,1)S(1)} copy-done((bf16[1,6144,256]{2,1,0:T(8,128)(2,1)S(1)}, bf16[1,6144,256]{2,1,0:T(8,128)(2,1)}, u32[]{:S(2)}) %copy-start.1) | copy-done | bytes 3145752
  74.3 1.9 %copy-done.2 = bf16[1,256,6144]{2,1,0:T(8,128)(2,1)S(1)} copy-done((bf16[1,256,6144]{2,1,0:T(8,128)(2,1)S(1)}, bf16[1,256,6144]{2,1,0:T(8,128)(2,1)}, u32[]{:S(2)}) %copy-start.2) | copy-done | bytes 3145752
  76.2 0.7 copy-done.6
  76.9 0.7 copy-done.9
  77.6 2.5 %shard_map.131 = (f32[16,24,192]{2,1,0:T(8,128)S(1)}, bf16[16,24,192]{2,1,0:T(8,128)(2,1)S(1)}) custom-call(s32[3]{0:T(128)S(1)} %copy-done.9, s32[8]{0:T(128)S(1)} %copy-done.11, bf16[16,24,256]{2,1,0:T(8,128)(2,1)S(1)} %all_to_all.28.own_ref, bf16[16,24,256]{2,1,0:T(8,128)(2,1)S(1)} %collective-permute-done.other_ref, f32[24,256]{1,0:T(8,128)S(1)} %copy-done.6, ...), custom_call_target="tpu_custom_call" | custom-call | tf_op jit(solution)/shard_map/pallas_call | solution.py:338
  80.1 0.0 copy-start.5
  80.1 0.7 copy-done.5
  80.8 0.1 collective-permute-start.1
  81.0 1.3 %collective-permute-done.1.got_ref = bf16[16,24,192]{2,1,0:T(8,128)(2,1)S(1)} collective-permute-done((bf16[16,24,192]{2,1,0:T(8,128)(2,1)S(1)}, bf16[16,24,192]{2,1,0:T(8,128)(2,1)S(1)}, u32[]{:S(2)}, u32[]{:S(2)}) %collective-permute-start.1) | collective-permute-done | bytes 147488 | tf_op jit(solution)/shard_map/ppermute | solution.py:286
  82.3 0.7 copy-done.12
  83.0 1.9 %shard_map.132 = bf16[128,3,192]{2,1,0:T(4,128)(2,1)} custom-call(f32[16,24,192]{2,1,0:T(8,128)} %copy-done.5, bf16[16,24,192]{2,1,0:T(8,128)(2,1)} %copy-done.12), custom_call_target="tpu_custom_call" | custom-call | tf_op jit(solution)/shard_map/pallas_call | solution.py:345
  84.9 21.9 %all_to_all.29.in_ref = bf16[128,3,192]{2,1,0:T(4,128)(2,1)} all-to-all(bf16[128,3,192]{2,1,0:T(4,128)(2,1)} %shard_map.132), channel_id=1, replica_groups=mesh['seq_0'=4,'seq_1'=4,'seq_2'=2,'exp'=8] {'seq_0','seq_1','exp'}, dimensions={0} | all-to-all | bytes 294912 | tf_op jit(solution)/shard_map/all_to_all | solution.py:282
  106.8 1.7 %shard_map.133 = bf16[3,192]{1,0:T(4,128)(2,1)} custom-call(s32[3]{0:T(128)} %copy-done.8, bf16[128,3,192]{2,1,0:T(4,128)(2,1)} %all_to_all.29.in_ref, f32[24,256]{1,0:T(8,128)} %get-tuple-element.14.residual_ref), custom_call_target="tpu_custom_call" | custom-call | tf_op jit(solution)/shard_map/pallas_call | solution.py:347
  (11 shorter events, 0.0 us)
Async XLA Ops:
  0.0 72.4 %copy-start = (bf16[1,6144,256]{2,1,0:T(8,128)(2,1)S(1)}, bf16[1,6144,256]{2,1,0:T(8,128)(2,1)}, u32[]{:S(2)}) copy-start(bf16[1,6144,256]{2,1,0:T(8,128)(2,1)} %param.23) | copy-start | bytes 9437188
  0.1 1.6 %copy-start.3 = (bf16[24,256,128]{2,1,0:T(8,128)(2,1)S(1)}, bf16[24,256,128]{2,1,0:T(8,128)(2,1)}, u32[]{:S(2)}) copy-start(bf16[24,256,128]{2,1,0:T(8,128)(2,1)} %k_any.1) | copy-start | bytes 4718596
  1.6 1.4 %copy-start.4 = (bf16[24,256,128]{2,1,0:T(8,128)(2,1)S(1)}, bf16[24,256,128]{2,1,0:T(8,128)(2,1)}, u32[]{:S(2)}) copy-start(bf16[24,256,128]{2,1,0:T(8,128)(2,1)} %v_any.1) | copy-start | bytes 4718596
  3.0 0.8 copy-start.7
  3.8 0.7 copy-start.10
  4.5 30.1 %copy-start.8 = (s32[3]{0:T(128)}, s32[3]{0:T(128)S(1)}, u32[]{:S(2)}) copy-start(s32[3]{0:T(128)S(1)} %pad_add_fusion.where_ref) | copy-start | bytes 40
  4.5 67.9 %copy-start.11 = (s32[8]{0:T(128)S(1)}, s32[8]{0:T(128)}, u32[]{:S(2)}) copy-start(s32[8]{0:T(128)} %capacity_ref.1) | copy-start | bytes 100
  70.9 1.4 %collective-permute-start = (bf16[16,24,256]{2,1,0:T(8,128)(2,1)S(1)}, bf16[16,24,256]{2,1,0:T(8,128)(2,1)S(1)}, u32[]{:S(2)}, u32[]{:S(2)}) collective-permute-start(bf16[16,24,256]{2,1,0:T(8,128)(2,1)S(1)} %all_to_all.28.own_ref), channel_id=1, source_target_pairs={{0,8},{8,0},{1,9},{9,1},{2,10},{10,2},{3,11},{11,3},{4,12},{12,4},... | collective-permute-start | bytes 589832 | tf_op jit(solution)/shard_map/ppermute | solution.py:286
  72.4 1.9 %copy-start.1 = (bf16[1,6144,256]{2,1,0:T(8,128)(2,1)S(1)}, bf16[1,6144,256]{2,1,0:T(8,128)(2,1)}, u32[]{:S(2)}) copy-start(bf16[1,6144,256]{2,1,0:T(8,128)(2,1)} %param.24) | copy-start | bytes 9437188
  74.3 1.9 %copy-start.2 = (bf16[1,256,6144]{2,1,0:T(8,128)(2,1)S(1)}, bf16[1,256,6144]{2,1,0:T(8,128)(2,1)}, u32[]{:S(2)}) copy-start(bf16[1,256,6144]{2,1,0:T(8,128)(2,1)} %param.25) | copy-start | bytes 9437188
  76.2 0.7 copy-start.6
  76.9 0.7 copy-start.9
  80.1 0.8 copy-start.5
  80.8 1.4 %collective-permute-start.1 = (bf16[16,24,192]{2,1,0:T(8,128)(2,1)S(1)}, bf16[16,24,192]{2,1,0:T(8,128)(2,1)S(1)}, u32[]{:S(2)}, u32[]{:S(2)}) collective-permute-start(bf16[16,24,192]{2,1,0:T(8,128)(2,1)S(1)} %get-tuple-element.16), channel_id=1, source_target_pairs={{0,8},{8,0},{1,9},{9,1},{2,10},{10,2},{3,11},{11,3},{4,12},{12,4},... | collective-permute-start | bytes 442376 | tf_op jit(solution)/shard_map/ppermute | solution.py:286
  82.3 0.7 copy-start.12

commit v2 on v1

--- a/solution.py
+++ b/solution.py
@@ -29,7 +29,7 @@
 bf16 = jnp.bfloat16
 VMEM = pl.BlockSpec(memory_space=pltpu.VMEM)
 SMEM = pl.BlockSpec(memory_space=pltpu.SMEM)
-ANY = pl.BlockSpec(memory_space=pl.ANY)
+HBM = pl.BlockSpec(memory_space=pltpu.HBM)
 
 
 def lanes(shape):
@@ -48,7 +48,11 @@
 PER = TOKENS // CHUNKS
 
 
-def attention_kernel(where_ref, lengths_ref, q_ref, k_any, v_any, out_ref, kbuf, vbuf, qs, sems):
+def attention_kernel(lengths_any, q_any, k_any, v_any, out_ref, lengths_ref, q_ref, kbuf, vbuf, qs, sems):
+    heads = pltpu.make_async_copy(q_any, q_ref, sems.at[2, 0])
+    limits = pltpu.make_async_copy(lengths_any, lengths_ref, sems.at[2, 1])
+    heads.start()
+    limits.start()
     copies = []
     for i in range(CHUNKS):
         part = pl.ds(i * PER, PER)
@@ -62,10 +66,12 @@
         pair[0].start()
         pair[1].start()
     qs[...] = jnp.zeros_like(qs)
+    heads.wait()
     for h in range(GROUP):
         qs[pl.ds(h, TOKENS, stride=SUB), :] = q_ref[:, h * HEAD_DIM : (h + 1) * HEAD_DIM].astype(f32)
-    first = where_ref[0]
+    limits.wait()
     span = k_any.shape[1]
+    first = lax.axis_index(SEQ) * span
     places = first + lanes((SUB, span))
     lane, sub = lanes((SUB, 128)), subs((SUB, 128))
     scale = 1.0 / math.sqrt(HEAD_DIM)
@@ -121,7 +127,7 @@
     return jnp.sum(jnp.where(lanes(shape) == subs(shape), wide, 0.0), axis=2, keepdims=True)
 
 
-def merge_kernel(in_ref, out_ref):
+def merge_kernel(in_ref, ahead_ref, out_ref):
     blocks = [in_ref[i].astype(f32).reshape(HALF, SUB, 128) for i in range(8)]
     peak, factors, total = combined(blocks)
     weighted = jnp.zeros((HALF, SUB, 128), f32)
@@ -138,7 +144,7 @@
         out_ref[i] = block
 
 
-def project_kernel(where_ref, ids_ref, in_ref, hidden_ref, weight_ref, out_ref, rest_ref, att, wide):
+def project_kernel(ids_ref, in_ref, hidden_ref, weight_ref, ahead_ref, out_ref, rest_ref, att, wide):
     for half in range(2):
         blocks = [in_ref[2 * z + half].astype(f32).reshape(HALF, SUB, 128) for z in range(4)]
         _, factors, total = combined(blocks)
@@ -156,7 +162,7 @@
             (((1,), (1,)), ((), ())),
             preferred_element_type=f32,
         )
-    mine = OWNED * where_ref[1]
+    mine = OWNED * lax.axis_index("exp")
     row = subs((TOKENS, COLS))
     hidden = hidden_ref[...].astype(f32)
     for r in range(OWNED):
@@ -178,7 +184,7 @@
     rest_ref[...] = jnp.where(owned, full - sent.astype(f32), 0.0)
 
 
-def gained_kernel(in_ref, rest_ref, gain_ref, router_ref, out_ref, residual_ref, wide):
+def gained_kernel(in_ref, rest_ref, gain_ref, router_ref, ahead_ref, out_ref, residual_ref, wide):
     total = rest_ref[...]
     for i in range(8):
         total += in_ref[i].astype(f32)
@@ -204,9 +210,9 @@
 
 
 def expert_kernel(
-    where_ref, capacity_ref, own_ref, other_ref, residual_ref, gate_ref, up_ref, down_ref, keep_ref, send_ref
+    capacity_ref, own_ref, other_ref, residual_ref, gate_ref, up_ref, down_ref, keep_ref, send_ref
 ):
-    core, me = where_ref[2], where_ref[1]
+    core, me = lax.axis_index("seq_2"), lax.axis_index("exp")
     stats = jnp.zeros((TOKENS, 128), f32)
     gate = jnp.zeros((TOKENS, 256), f32)
     up = jnp.zeros((TOKENS, 256), f32)
@@ -253,8 +259,8 @@
             out_ref[EXPERTS * k + e] = total[OWNED * e : OWNED * (e + 1), :].astype(bf16)
 
 
-def final_kernel(where_ref, in_ref, residual_ref, out_ref):
-    me = where_ref[1]
+def final_kernel(in_ref, residual_ref, out_ref):
+    me = lax.axis_index("exp")
     total = jnp.zeros((OWNED, COLS), f32)
     for e in range(EXPERTS):
         rows = residual_ref[OWNED * e : OWNED * (e + 1), :COLS]
@@ -266,7 +272,7 @@
     return jax.ShapeDtypeStruct(shape, dtype)
 
 
-def call(kernel, outs, specs, scratch=(), limit=None):
+def call(kernel, outs, specs, scratch=(), limit=6 << 20):
     single = not isinstance(outs, tuple)
     return pl.pallas_call(
         kernel,
@@ -275,6 +281,7 @@
         out_specs=VMEM if single else (VMEM,) * len(outs),
         scratch_shapes=list(scratch),
         compiler_params=pltpu.CompilerParams(vmem_limit_bytes=limit),
+        cost_estimate=pl.CostEstimate(flops=1 << 20, bytes_accessed=1 << 20, transcendentals=0),
     )
 
 
@@ -301,50 +308,48 @@
     w_up,
     w_down,
 ):
-    span = key_cache.shape[1]
-    where = jnp.stack(
-        [lax.axis_index(SEQ) * span, lax.axis_index("exp"), lax.axis_index("seq_2")]
-    ).astype(jnp.int32)
     partial = call(
         attention_kernel,
         shaped((8, HALF_ROWS, 128), bf16),
-        (SMEM, SMEM, VMEM, ANY, ANY),
+        (HBM, HBM, HBM, HBM),
         (
+            pltpu.SMEM(lengths.shape, jnp.int32),
+            pltpu.VMEM(queries.shape, bf16),
             pltpu.VMEM(key_cache.shape, bf16),
             pltpu.VMEM(value_cache.shape, bf16),
             pltpu.VMEM((TOKENS * SUB, 128), f32),
-            pltpu.SemaphoreType.DMA((2, CHUNKS)),
+            pltpu.SemaphoreType.DMA((3, CHUNKS)),
         ),
-        limit=12 << 20,
-    )(where, lengths, queries, key_cache, value_cache)
+        limit=60 << 20,
+    )(lengths, queries, key_cache, value_cache)
     partial = exchanged(partial, ("seq_0", "seq_2"))
-    partial = call(merge_kernel, shaped((8, HALF_ROWS, 128), bf16), (VMEM,))(partial)
+    partial = call(merge_kernel, shaped((8, HALF_ROWS, 128), bf16), (VMEM, VMEM))(partial, w_gate)
     partial = exchanged(partial, ("seq_1", "seq_2"))
     projected, rest = call(
         project_kernel,
         (shaped((8, TOKENS, 256), bf16), shaped((TOKENS, 256), f32)),
-        (SMEM, SMEM, VMEM, VMEM, VMEM),
+        (SMEM, VMEM, VMEM, VMEM, VMEM),
         (pltpu.VMEM((TOKENS * SUB, 128), f32), pltpu.VMEM((TOKENS, 256), f32)),
-    )(where, expert_ids.T, partial, hidden_in, out_weight.T)
+    )(expert_ids.T, partial, hidden_in, out_weight.T, w_up)
     projected = exchanged(projected, "exp")
     gained, residual = call(
         gained_kernel,
         (shaped((CHIPS, TOKENS, 256), bf16), shaped((TOKENS, 256), f32)),
-        (VMEM,) * 4,
+        (VMEM,) * 5,
         (pltpu.VMEM((TOKENS, 256), f32),),
-    )(projected, rest, norm_gain[None, :], router.T)
+    )(projected, rest, norm_gain[None, :], router.T, w_down)
     own = exchanged(gained, ("seq_0", "seq_1"))
     other = swapped(own)
     keep, send = call(
         expert_kernel,
         (shaped((CHIPS, TOKENS, COLS), f32), shaped((CHIPS, TOKENS, COLS), bf16)),
-        (SMEM, SMEM) + (VMEM,) * 6,
-        limit=24 << 20,
-    )(where, capacity, own, other, residual, w_gate[0], w_up[0], w_down[0])
+        (SMEM,) + (VMEM,) * 6,
+        limit=14 << 20,
+    )(capacity, own, other, residual, w_gate[0], w_up[0], w_down[0])
     got = swapped(send)
     summed = call(pair_kernel, shaped((CHIPS * EXPERTS, OWNED, COLS), bf16), (VMEM, VMEM))(keep, got)
     summed = exchanged(summed, ("seq_0", "seq_1", "exp"))
-    return call(final_kernel, shaped((OWNED, COLS), bf16), (SMEM, VMEM, VMEM))(where, summed, residual)
+    return call(final_kernel, shaped((OWNED, COLS), bf16), (VMEM, VMEM))(summed, residual)
 
 
 def solution(mesh):

time: 109 us -> 87.9 us (0.81)
  local copies, waits for them, and re-layouts: 11 us -> 0.04 us
  Pallas kernels: 16.4 us -> 9.12 us
  blocking collectives: 78.1 us -> 75.4 us
    unnamed x26 -> x18, local copies, waits for them, and re-layouts: 11 us -> 0.04 us
    pallas_call x3, Pallas kernels: 7.72 us -> 4.97 us  [the longest x1 3.81 us: on_device(): call(attention_kernel, shaped((8, HALF_ROWS, 128), bf16), (HBM, HBM, HBM,...]
    all_to_all x5, blocking collectives: 78.1 us -> 75.4 us  [exchanged(): return lax.all_to_all(value, axes, 0, 0, tiled=True)]
    pallas_call x1, Pallas kernels: 1.92 us -> 0.18 us  [on_device(): call(pair_kernel, shaped((CHIPS * EXPERTS, OWNED, COLS), bf16), (VMEM, VM...]
    pallas_call x1, Pallas kernels: 1.82 us -> 0.23 us  [on_device(): call(gained_kernel, (shaped((CHIPS, TOKENS, 256), bf16), shaped((TOKENS,...]
    pallas_call x1, Pallas kernels: 2.38 us -> 1.2 us  [on_device(): call(project_kernel, (shaped((8, TOKENS, 256), bf16), shaped((TOKENS, 256...]
where the time goes in v2:
time: 87.9 us; the launch traced here: 87.6 us
  blocking collectives  75.4 us (86%)
  Pallas kernels  9.12 us (10%)
  waiting for transfers between devices  2.74 us (3%)
    all_to_all x5, blocking collectives, exchanged(): return lax.all_to_all(value, axes, 0, 0, tiled=True)  75.4 us
    pallas_call x1, Pallas kernels, on_device(): call(attention_kernel, shaped((8, HALF_ROWS, 128), bf16), (HBM, HBM, HBM,...  3.81 us
    ppermute x2, waiting for transfers between devices, swapped(): return lax.ppermute(value, 'seq_2', [(0, 1), (1, 0)])  2.74 us
    pallas_call x1, Pallas kernels, on_device(): call(expert_kernel, (shaped((CHIPS, TOKENS, COLS), f32), shaped((CHIPS, T...  2.54 us
  transfers between devices with their start and end apart: 2, of which 2 were waited for; matrix products, arithmetic and copies ran while one was open for 0% of the time, Pallas kernels for 0%

profile of v2, /device:TPU:32, one launch (start us, length us, event | category | flops | bytes accessed | tf_op | source)
XLA Modules:
  0.0 87.6 jit_solution(6300559380286954903)
XLA Ops:
  0.0 0.0 copy-start
  0.0 0.0 copy-start.7
  0.0 0.0 copy-start.3
  0.0 0.0 copy-start.5
  0.0 3.8 %shard_map.127 = bf16[8,96,128]{2,1,0:T(8,128)(2,1)} custom-call(s32[24]{0:T(128)} %lengths_any.1, bf16[24,768]{1,0:T(8,128)(2,1)} %q_any.1, bf16[24,256,128]{2,1,0:T(8,128)(2,1)} %k_any.1, bf16[24,256,128]{2,1,0:T(8,128)(2,1)} %v_any.1), custom_call_target="tpu_custom_call" | custom-call | flops 1048576 | bytes 1048576 | tf_op jit(solution)/shard_map/pallas_call | solution.py:311
  3.8 0.0 copy-start.2
  3.9 11.6 %all_to_all.25.in_ref = bf16[8,96,128]{2,1,0:T(8,128)(2,1)S(1)} all-to-all(bf16[8,96,128]{2,1,0:T(8,128)(2,1)} %shard_map.127), channel_id=1, replica_groups=mesh['seq_0'=4,'seq_1'=4,'seq_2'=2,'exp'=8] {'seq_0','seq_2'}, dimensions={0} | all-to-all | bytes 393216 | tf_op jit(solution)/shard_map/all_to_all | solution.py:289
  15.4 0.0 copy-done
  15.4 0.0 copy-start.1
  15.4 0.4 shard_map.128
  15.9 12.7 %all_to_all.26.in_ref = bf16[8,96,128]{2,1,0:T(8,128)(2,1)S(1)} all-to-all(bf16[8,96,128]{2,1,0:T(8,128)(2,1)S(1)} %shard_map.128), channel_id=1, replica_groups=mesh['seq_0'=4,'seq_1'=4,'seq_2'=2,'exp'=8] {'seq_1','seq_2'}, dimensions={0} | all-to-all | bytes 393216 | tf_op jit(solution)/shard_map/all_to_all | solution.py:289
  28.6 0.0 copy-done.7
  28.6 0.0 copy-done.3
  28.6 0.0 copy-done.5
  28.6 0.0 copy-done.2
  28.6 0.0 copy-start.8
  28.6 1.2 %shard_map.129 = (bf16[8,24,256]{2,1,0:T(8,128)(2,1)S(1)}, f32[24,256]{1,0:T(8,128)S(1)}) custom-call(s32[2,3]{1,0:T(2,128)S(1)} %bitcast.13, bf16[8,96,128]{2,1,0:T(8,128)(2,1)S(1)} %all_to_all.26.in_ref, bf16[3,192]{1,0:T(4,128)(2,1)S(1)} %copy-done.5, bf16[192,768]{1,0:T(8,128)(2,1)S(1)} %bitcast.10, bf16[1,6144,256]{2,1,0:T(8,128)(2,1)S(1)} %copy-done.2), custom_call_target="tpu_custom_call" | custom-call | flops 1048576 | bytes 1048576 | tf_op jit(solution)/shard_map/pallas_call | solution.py:328
  29.8 18.6 %all_to_all.27.in_ref = bf16[8,24,256]{2,1,0:T(8,128)(2,1)S(1)} all-to-all(bf16[8,24,256]{2,1,0:T(8,128)(2,1)S(1)} %get-tuple-element.11), channel_id=1, replica_groups=mesh['seq_0'=4,'seq_1'=4,'seq_2'=2,'exp'=8] {'exp'}, dimensions={0} | all-to-all | bytes 196608 | tf_op jit(solution)/shard_map/all_to_all | solution.py:289
  48.3 0.0 copy-done.1
  48.3 0.0 copy-done.4
  48.4 0.0 copy-done.6
  48.4 0.2 shard_map.130
  48.6 12.2 %all_to_all.28.own_ref = bf16[16,24,256]{2,1,0:T(8,128)(2,1)S(1)} all-to-all(bf16[16,24,256]{2,1,0:T(8,128)(2,1)S(1)} %get-tuple-element.13), channel_id=1, replica_groups=mesh['seq_0'=4,'seq_1'=4,'seq_2'=2,'exp'=8] {'seq_0','seq_1'}, dimensions={0} | all-to-all | bytes 393216 | tf_op jit(solution)/shard_map/all_to_all | solution.py:289
  60.8 0.0 collective-permute-start
  60.8 1.4 %collective-permute-done.other_ref = bf16[16,24,256]{2,1,0:T(8,128)(2,1)S(1)} collective-permute-done((bf16[16,24,256]{2,1,0:T(8,128)(2,1)S(1)}, bf16[16,24,256]{2,1,0:T(8,128)(2,1)S(1)}, u32[]{:S(2)}, u32[]{:S(2)}) %collective-permute-start) | collective-permute-done | bytes 196640 | tf_op jit(solution)/shard_map/ppermute | solution.py:293
  62.2 0.0 copy-done.8
  62.2 2.5 %shard_map.131 = (f32[16,24,192]{2,1,0:T(8,128)S(1)}, bf16[16,24,192]{2,1,0:T(8,128)(2,1)S(1)}) custom-call(s32[8]{0:T(128)S(1)} %copy-done.8, bf16[16,24,256]{2,1,0:T(8,128)(2,1)S(1)} %all_to_all.28.own_ref, bf16[16,24,256]{2,1,0:T(8,128)(2,1)S(1)} %collective-permute-done.other_ref, f32[24,256]{1,0:T(8,128)S(1)} %get-tuple-element.14.residual_ref, ...), custom_call_target="tpu_custom_call" | custom-call | flops 1048576 | bytes 1048576 | tf_op jit(solution)/shard_map/pallas_call | solution.py:343
  64.8 0.2 collective-permute-start.1
  65.0 1.3 %collective-permute-done.1.got_ref = bf16[16,24,192]{2,1,0:T(8,128)(2,1)S(1)} collective-permute-done((bf16[16,24,192]{2,1,0:T(8,128)(2,1)S(1)}, bf16[16,24,192]{2,1,0:T(8,128)(2,1)S(1)}, u32[]{:S(2)}, u32[]{:S(2)}) %collective-permute-start.1) | collective-permute-done | bytes 147488 | tf_op jit(solution)/shard_map/ppermute | solution.py:293
  66.3 0.2 shard_map.132
  66.5 20.4 %all_to_all.29.in_ref = bf16[128,3,192]{2,1,0:T(4,128)(2,1)S(1)} all-to-all(bf16[128,3,192]{2,1,0:T(4,128)(2,1)S(1)} %shard_map.132), channel_id=1, replica_groups=mesh['seq_0'=4,'seq_1'=4,'seq_2'=2,'exp'=8] {'seq_0','seq_1','exp'}, dimensions={0} | all-to-all | bytes 294912 | tf_op jit(solution)/shard_map/all_to_all | solution.py:289
  86.9 0.7 shard_map.133
  (2 shorter events, 0.0 us)
Async XLA Ops:
  0.0 15.4 %copy-start = (bf16[1,6144,256]{2,1,0:T(8,128)(2,1)S(1)}, bf16[1,6144,256]{2,1,0:T(8,128)(2,1)}, u32[]{:S(2)}) copy-start(bf16[1,6144,256]{2,1,0:T(8,128)(2,1)} %ahead_ref.3) | copy-start | bytes 9437188
  0.0 28.6 %copy-start.7 = (s32[3,2]{0,1:T(2,128)S(1)}, s32[3,2]{0,1:T(2,128)}, u32[]{:S(2)}) copy-start(s32[3,2]{0,1:T(2,128)} %param.21) | copy-start | bytes 76
  0.0 28.6 %copy-start.3 = (bf16[768,192]{0,1:T(8,128)(2,1)S(1)}, bf16[768,192]{0,1:T(8,128)(2,1)}, u32[]{:S(2)}) copy-start(bf16[768,192]{0,1:T(8,128)(2,1)} %param.18) | copy-start | bytes 884740
  0.0 28.6 %copy-start.5 = (bf16[3,192]{1,0:T(4,128)(2,1)S(1)}, bf16[3,192]{1,0:T(4,128)(2,1)}, u32[]{:S(2)}) copy-start(bf16[3,192]{1,0:T(4,128)(2,1)} %hidden_ref.1) | copy-start | bytes 3460
  3.8 24.7 %copy-start.2 = (bf16[1,6144,256]{2,1,0:T(8,128)(2,1)S(1)}, bf16[1,6144,256]{2,1,0:T(8,128)(2,1)}, u32[]{:S(2)}) copy-start(bf16[1,6144,256]{2,1,0:T(8,128)(2,1)} %ahead_ref.4) | copy-start | bytes 9437188
  15.4 32.9 %copy-start.1 = (bf16[1,256,6144]{2,1,0:T(8,128)(2,1)S(1)}, bf16[1,256,6144]{2,1,0:T(8,128)(2,1)}, u32[]{:S(2)}) copy-start(bf16[1,256,6144]{2,1,0:T(8,128)(2,1)} %ahead_ref.5) | copy-start | bytes 9437188
  15.4 32.9 %copy-start.4 = (bf16[192,8]{0,1:T(8,128)(2,1)S(1)}, bf16[192,8]{0,1:T(8,128)(2,1)}, u32[]{:S(2)}) copy-start(bf16[192,8]{0,1:T(8,128)(2,1)} %param.20) | copy-start | bytes 9220
  15.4 32.9 %copy-start.6 = (f32[192]{0:T(256)S(1)}, f32[192]{0:T(256)}, u32[]{:S(2)}) copy-start(f32[192]{0:T(256)} %param.19) | copy-start | bytes 2308
  28.6 33.6 %copy-start.8 = (s32[8]{0:T(128)S(1)}, s32[8]{0:T(128)}, u32[]{:S(2)}) copy-start(s32[8]{0:T(128)} %capacity_ref.1) | copy-start | bytes 100
  60.8 1.4 %collective-permute-start = (bf16[16,24,256]{2,1,0:T(8,128)(2,1)S(1)}, bf16[16,24,256]{2,1,0:T(8,128)(2,1)S(1)}, u32[]{:S(2)}, u32[]{:S(2)}) collective-permute-start(bf16[16,24,256]{2,1,0:T(8,128)(2,1)S(1)} %all_to_all.28.own_ref), channel_id=1, source_target_pairs={{0,8},{8,0},{1,9},{9,1},{2,10},{10,2},{3,11},{11,3},{4,12},{12,4},... | collective-permute-start | bytes 589832 | tf_op jit(solution)/shard_map/ppermute | solution.py:293
  64.8 1.5 %collective-permute-start.1 = (bf16[16,24,192]{2,1,0:T(8,128)(2,1)S(1)}, bf16[16,24,192]{2,1,0:T(8,128)(2,1)S(1)}, u32[]{:S(2)}, u32[]{:S(2)}) collective-permute-start(bf16[16,24,192]{2,1,0:T(8,128)(2,1)S(1)} %get-tuple-element.16), channel_id=1, source_target_pairs={{0,8},{8,0},{1,9},{9,1},{2,10},{10,2},{3,11},{11,3},{4,12},{12,4},... | collective-permute-start | bytes 442376 | tf_op jit(solution)/shard_map/ppermute | solution.py:293

commit v3 on v2

v3 whole, which is shorter than its diff:
```python
import functools
import math

import jax
import jax.numpy as jnp
from jax import lax
from jax.experimental import pallas as pl
from jax.experimental.pallas import tpu as pltpu
from jax.sharding import Mesh
from jax.sharding import PartitionSpec as P

D = 6144
HEADS = 48
KV_HEADS = 8
HEAD_DIM = 128
EXPERTS = 8
TOKENS = 24
OWNED = 3
GROUP = HEADS // KV_HEADS
COLS = 192
HALF = TOKENS // 2
SUB = 8
HALF_ROWS = HALF * SUB
CHIPS = 16
SEQ = ("seq_0", "seq_1", "seq_2")
masked_score = -1e30
norm_eps = 1e-05
f32 = jnp.float32
bf16 = jnp.bfloat16
VMEM = pl.BlockSpec(memory_space=pltpu.VMEM)
SMEM = pl.BlockSpec(memory_space=pltpu.SMEM)
HBM = pl.BlockSpec(memory_space=pltpu.HBM)


def lanes(shape):
    return lax.broadcasted_iota(jnp.int32, shape, len(shape) - 1)


def subs(shape):
    return lax.broadcasted_iota(jnp.int32, shape, len(shape) - 2)


def rounded(x):
    return x.astype(bf16).astype(f32)


CHUNKS = 4
PER = TOKENS // CHUNKS
BOTH = 2 * COLS
PACKED = HALF * GROUP
BLOCK = PACKED + SUB
ROWS = 16


def attention_kernel(
    lengths_any, q_any, k_any, v_any, hidden_ref, router_ref, gain_ref,
    keep_ref, send_ref, small_ref,
    lengths_ref, q_ref, kbuf, vbuf, qs, halves, sems,
):
    heads = pltpu.make_async_copy(q_any, q_ref, sems.at[2, 0])
    limits = pltpu.make_async_copy(lengths_any, lengths_ref, sems.at[2, 1])
    heads.start()
    limits.start()
    copies = []
    for i in range(CHUNKS):
        part = pl.ds(i * PER, PER)
        copies.append(
            (
                pltpu.make_async_copy(k_any.at[part], kbuf.at[part], sems.at[0, i]),
                pltpu.make_async_copy(v_any.at[part], vbuf.at[part], sems.at[1, i]),
            )
        )
    for pair in copies:
        pair[0].start()
        pair[1].start()
    gain = gain_ref[...]
    gain_hi = rounded(gain)
    gain_mid = rounded(gain - gain_hi)
    row = subs((ROWS, COLS))
    small = jnp.zeros((ROWS, COLS), f32)
    hidden, router = hidden_ref[...].astype(f32), router_ref[...].astype(f32)
    lines = [hidden[r : r + 1] for r in range(OWNED)] + [router[r : r + 1] for r in range(EXPERTS)]
    for r, line in enumerate(lines + [gain_hi, gain_mid, gain - gain_hi - gain_mid]):
        small = jnp.where(row == r, line, small)
    small_ref[...] = small.astype(bf16)
    qs[...] = jnp.zeros_like(qs)
    heads.wait()
    for h in range(GROUP):
        qs[pl.ds(h, TOKENS, stride=SUB), :] = q_ref[:, h * HEAD_DIM : (h + 1) * HEAD_DIM].astype(f32)
    limits.wait()
    span = k_any.shape[1]
    first = lax.axis_index(SEQ) * span
    places = first + lanes((SUB, span))
    lane, sub = lanes((SUB, 128)), subs((SUB, 128))
    scale = 1.0 / math.sqrt(HEAD_DIM)
    for i in range(CHUNKS):
        copies[i][0].wait()
        scores = []
        for b in range(i * PER, (i + 1) * PER):
            query = qs[b * SUB : (b + 1) * SUB, :].astype(bf16)
            s = lax.dot_general(query, kbuf[b], (((1,), (1,)), ((), ())), preferred_element_type=f32)
            scores.append(jnp.where(places < lengths_ref[b], s * scale, masked_score))
        copies[i][1].wait()
        for n, b in enumerate(range(i * PER, (i + 1) * PER)):
            s = scores[n]
            peak = rounded(jnp.max(s, axis=-1, keepdims=True))
            p = jnp.where(places < lengths_ref[b], jnp.exp(s - peak), 0.0)
            total = jnp.sum(p, axis=-1, keepdims=True)
            p_hi = rounded(p)
            both = jnp.concatenate([p_hi, p - p_hi], axis=0).astype(bf16)
            weighted = jnp.dot(both, vbuf[b], preferred_element_type=f32)
            weighted = weighted[:SUB] + weighted[SUB:]
            stats = jnp.where(lane == sub, peak, 0.0)
            stats = jnp.where(lane == sub + SUB, total, stats)
            stats = jnp.sum(jnp.where(sub < GROUP, stats, 0.0), axis=0, keepdims=True)
            half, line = b // HALF, (b % HALF) * SUB
            halves[half, line : line + SUB, :] = jnp.where(sub == GROUP, stats, weighted)
    core = lax.axis_index("seq_2")
    keep_ref[...] = halves[core]
    send_ref[...] = halves[1 - core]


def as_column(x):
    shape = (HALF, SUB, 128)
    wide = jnp.broadcast_to(x, shape)
    return jnp.sum(jnp.where(lanes(shape) == subs(shape), wide, 0.0), axis=2, keepdims=True)


def merge_kernel(keep_ref, got_ref, weight_ref, small_ref, ahead_ref, out_ref, packed):
    shape = (HALF, SUB, 128)
    sub = subs(shape)
    blocks = [ref[...].reshape(shape) for ref in (keep_ref, got_ref)]
    stats = [jnp.sum(jnp.where(sub == GROUP, x, 0.0), axis=1, keepdims=True) for x in blocks]
    peak = jnp.maximum(stats[0], stats[1])
    weighted, total = jnp.zeros(shape, f32), jnp.zeros((HALF, 1, 128), f32)
    for x, s in zip(blocks, stats):
        factor = jnp.exp(jnp.minimum(s - peak, 0.0))
        total += factor * pltpu.roll(s, 128 - SUB, 2)
        weighted += as_column(factor) * x
    flat = lanes((HALF, 1, 128))
    total_hi = rounded(total)
    line = jnp.where(flat < SUB, peak, pltpu.roll(total_hi, SUB, 2))
    line = jnp.where(flat < 2 * SUB, line, pltpu.roll(total - total_hi, 2 * SUB, 2))
    line = jnp.where(flat % SUB < GROUP, jnp.where(flat < 3 * SUB, line, 0.0), 0.0)
    tile, row, lane = jnp.zeros((SUB, 128), f32), subs((SUB, 128)), lanes((SUB, 128))
    for t in range(HALF):
        packed[GROUP * t : GROUP * (t + 1), :] = weighted[t, :GROUP, :]
        here = (row == t % SUB) & (lane // 32 == t // SUB)
        value = line[t] if t < SUB else pltpu.roll(line[t], 32, 1)
        tile = jnp.where(here, value, tile)
    packed[PACKED:, :] = tile
    block = packed[...].astype(bf16)
    for i in range(CHIPS):
        out_ref[i] = block


def project_kernel(
    ids_ref, in_ref, hidden_ref, small_ref, weight_ref, other_ref, ahead_ref, out_ref, rest_ref, att, wide
):
    core, me = lax.axis_index("seq_2"), lax.axis_index("exp")
    tiles = [in_ref[i, PACKED:, :].astype(f32) for i in range(CHIPS)]
    peak = functools.reduce(jnp.maximum, tiles)
    factors = [jnp.exp(jnp.minimum(s - peak, 0.0)) for s in tiles]
    total = jnp.zeros((SUB, 128), f32)
    for s, factor in zip(tiles, factors):
        total += factor * (pltpu.roll(s, 128 - SUB, 1) + pltpu.roll(s, 128 - 2 * SUB, 1))
    lane = lanes((SUB, 128))
    inverse = 1.0 / jnp.where((lane % 32 < GROUP) & (total > 0.0), total, 1.0)
    row = lax.broadcasted_iota(jnp.int32, (PACKED, 2 * SUB), 0)
    column = lax.broadcasted_iota(jnp.int32, (PACKED, 2 * SUB), 1)
    spread = jnp.where((row // GROUP) % SUB == column % SUB, 1.0, 0.0).astype(bf16)
    row = subs((PACKED, 128))
    wanted = lanes((PACKED, 128)) == 32 * (row // GROUP // SUB) + row % GROUP
    weighted = jnp.zeros((PACKED, 128), f32)
    for i in range(CHIPS):
        factor = factors[i] * inverse
        factor_hi = rounded(factor)
        parts = jnp.concatenate([factor_hi, factor - factor_hi], axis=0).astype(bf16)
        wide_factor = jnp.dot(spread, parts, preferred_element_type=f32)
        factor = jnp.sum(jnp.where(wanted, wide_factor, 0.0), axis=-1, keepdims=True)
        weighted += factor * in_ref[i, :PACKED, :].astype(f32)
    att[:PACKED, :] = weighted
    acc, acc_other = jnp.zeros((HALF, COLS), f32), jnp.zeros((HALF, COLS), f32)
    over_features = (((1,), (1,)), ((), ()))
    for h in range(GROUP):
        rows = att[pl.ds(h, HALF, stride=GROUP), :].astype(bf16)
        cols = slice(h * HEAD_DIM, (h + 1) * HEAD_DIM)
        acc += lax.dot_general(rows, weight_ref[:, cols], over_features, preferred_element_type=f32)
        acc_other += lax.dot_general(rows, other_ref[:, cols], over_features, preferred_element_type=f32)
    mine = OWNED * me - HALF * core
    row = subs((HALF, COLS))
    hidden, hidden_other = hidden_ref[...].astype(f32), small_ref[...].astype(f32)
    for r in range(OWNED):
        acc += jnp.where(row == mine + r, hidden[r : r + 1, :], 0.0)
        acc_other += jnp.where(row == mine + r, hidden_other[r : r + 1, :], 0.0)
    row, lane = subs((ROWS, BOTH)), lanes((ROWS, BOTH))
    ids = jnp.zeros((ROWS, BOTH), f32)
    for r in range(OWNED):
        for k in range(2):
            here = (row == HALF) & (lane == 2 * (OWNED * me + r) + k)
            ids = jnp.where(here, ids_ref[k, r].astype(f32), ids)
    wide[...] = ids
    wide[:HALF, :COLS] = jnp.where(core == 0, acc, acc_other)
    wide[:HALF, COLS:] = jnp.where(core == 0, acc_other, acc)
    full = wide[...]
    sent = full.astype(bf16)
    for i in range(EXPERTS):
        out_ref[i] = sent
    owned = (row >= mine) & (row < mine + OWNED) & (row < HALF)
    rest_ref[...] = jnp.where(owned, full - sent.astype(f32), 0.0)


def gained_kernel(in_ref, rest_ref, gain_ref, router_ref, small_ref, ahead_ref, out_ref, residual_ref, wide):
    core = lax.axis_index("seq_2")
    total = rest_ref[...]
    for i in range(EXPERTS):
        total += in_ref[i].astype(f32)
    residual_ref[...] = total
    small = small_ref[...].astype(f32)
    router, router_other = router_ref[...].astype(f32), small[OWNED : OWNED + EXPERTS]
    gain = gain_ref[...]
    gain_other = small[11:12] + (small[12:13] + small[13:14])
    wide[:EXPERTS, :COLS] = jnp.where(core == 0, router, router_other)
    wide[:EXPERTS, COLS:] = jnp.where(core == 0, router_other, router)
    wide[EXPERTS : EXPERTS + 1, :COLS] = jnp.where(core == 0, gain, gain_other)
    wide[EXPERTS : EXPERTS + 1, COLS:] = jnp.where(core == 0, gain_other, gain)
    routers = wide[:EXPERTS, :].astype(bf16)
    row = subs((ROWS, BOTH))
    residual = jnp.where(row < HALF, total, 0.0)
    gained = residual * wide[EXPERTS : EXPERTS + 1, :]
    hi = gained.astype(bf16)
    lo = (gained - hi.astype(f32)).astype(bf16)
    over_features = (((1,), (1,)), ((), ()))
    logits = lax.dot_general(hi, routers, over_features, preferred_element_type=f32)
    logits += lax.dot_general(lo, routers, over_features, preferred_element_type=f32)
    squares = jnp.sum(residual * residual, axis=-1, keepdims=True)
    logits_hi, squares_hi = rounded(logits), rounded(squares)
    wide[:, :128] = jnp.zeros((ROWS, 128), f32)
    wide[:, :8] = logits_hi
    wide[:, 8:9] = squares_hi
    wide[:, 16:24] = logits - logits_hi
    wide[:, 24:25] = squares - squares_hi
    stats = wide[:, :128].astype(bf16)
    to = lax.broadcasted_iota(jnp.int32, (ROWS, ROWS), 0)
    source = lax.broadcasted_iota(jnp.int32, (ROWS, ROWS), 1)
    row = subs((ROWS, 128))
    for j in range(3):
        choice = jnp.where((to >= HALF) & (source == 3 * (to - HALF) + j), 1.0, 0.0).astype(bf16)
        packed = jnp.dot(choice, stats, preferred_element_type=f32)
        cols = slice(128 * j, 128 * (j + 1))
        sent = jnp.where(row < HALF, gained[:, cols], packed).astype(bf16)
        for i in range(CHIPS):
            out_ref[i, :, cols] = sent


def expert_kernel(
    capacity_ref, own_ref, other_ref, residual_ref, gate_ref, up_ref, down_ref, keep_ref, send_ref
):
    core, me = lax.axis_index("seq_2"), lax.axis_index("exp")
    sums = [jnp.zeros((ROWS, BOTH), f32) for _ in range(2)]
    gate = jnp.zeros((2 * ROWS, 256), f32)
    up = jnp.zeros((2 * ROWS, 256), f32)
    for k in range(CHIPS):
        own, other = own_ref[k], other_ref[k]
        pair = (jnp.where(core == 0, own, other), jnp.where(core == 0, other, own))
        for i in range(2):
            sums[i] += pair[i].astype(f32)
        x = jnp.concatenate(pair, axis=0)
        rows = slice(BOTH * k, BOTH * (k + 1))
        gate += jnp.dot(x, gate_ref[rows, :], preferred_element_type=f32)
        up += jnp.dot(x, up_ref[rows, :], preferred_element_type=f32)
    shape = (2 * ROWS, 128)
    lane, row = lanes(shape), subs(shape)
    stats = jnp.zeros(shape, f32)
    for half in range(2):
        for t in range(HALF):
            line = sums[half][HALF + t // 3 : HALF + t // 3 + 1, 128 * (t % 3) : 128 * (t % 3 + 1)]
            stats = jnp.where(row == ROWS * half + t, line, stats)
    stats += pltpu.roll(stats, 128 - 16, 1)

    def pick(x, place):
        return jnp.sum(jnp.where(lane == place, x, 0.0), axis=-1, keepdims=True)

    scale = lax.rsqrt(pick(stats, 8) / D + norm_eps)
    logits = stats * scale
    inside = row % ROWS
    token = HALF * (row // ROWS) + inside
    named = jnp.broadcast_to(residual_ref[HALF : HALF + 1, :128], shape)
    first, second = pick(named, 2 * token).astype(jnp.int32), pick(named, 2 * token + 1).astype(jnp.int32)
    names = (first == me) | (second == me)
    other = jnp.where(first == me, second, first)
    routed = 1.0 / (1.0 + jnp.exp(pick(logits, other) - pick(logits, me)))
    naming = jnp.broadcast_to(jnp.where(names, 1.0, 0.0), shape)
    place = inside % OWNED
    earlier = jnp.where(place >= 1, pltpu.roll(naming, 1, 0), 0.0)
    earlier += jnp.where(place >= 2, pltpu.roll(naming, 2, 0), 0.0)
    kept = names & (earlier[:, :1] < capacity_ref[me].astype(f32)) & (inside[:, :1] < HALF)
    weight = jnp.where(kept, routed, 0.0)
    gate, up = gate * scale, up * scale
    inner = (gate / (1.0 + jnp.exp(-gate)) * up * weight).astype(bf16)
    for k in range(CHIPS):
        y = jnp.dot(inner, down_ref[:, BOTH * k : BOTH * (k + 1)], preferred_element_type=f32)
        even, odd = y[:, :COLS], y[:, COLS:]
        keep_ref[k] = jnp.where(core == 0, even, odd)
        send_ref[k] = jnp.where(core == 0, odd, even).astype(bf16)
    residual = residual_ref[...]
    residual = jnp.where(core == 0, residual[:, COLS:], residual[:, :COLS])
    residual_hi = residual.astype(bf16)
    send_ref[CHIPS, :ROWS, :] = residual_hi
    send_ref[CHIPS, ROWS:, :] = (residual - residual_hi.astype(f32)).astype(bf16)


def pair_kernel(keep_ref, got_ref, out_ref):
    for k in range(CHIPS):
        total = keep_ref[k] + got_ref[k].astype(f32)
        for e in range(EXPERTS):
            line = ROWS * (e // 4) + OWNED * (e % 4)
            out_ref[EXPERTS * k + e] = total[line : line + OWNED, :].astype(bf16)


def final_kernel(in_ref, residual_ref, got_ref, out_ref):
    core, me = lax.axis_index("seq_2"), lax.axis_index("exp")
    residual = residual_ref[...]
    own = jnp.where(core == 0, residual[:, :COLS], residual[:, COLS:])
    got = got_ref[CHIPS].astype(f32)
    residual = jnp.where(me // 4 == core, own, got[:ROWS] + got[ROWS:])
    total = jnp.zeros((OWNED, COLS), f32)
    for q in range(4):
        total += jnp.where(me % 4 == q, residual[OWNED * q : OWNED * (q + 1), :], 0.0)
    out_ref[...] = (total + jnp.sum(in_ref[...].astype(f32), axis=0)).astype(bf16)


def shaped(shape, dtype):
    return jax.ShapeDtypeStruct(shape, dtype)


def call(kernel, outs, specs, scratch=(), limit=6 << 20):
    single = not isinstance(outs, tuple)
    return pl.pallas_call(
        kernel,
        out_shape=outs,
        in_specs=list(specs),
        out_specs=VMEM if single else (VMEM,) * len(outs),
        scratch_shapes=list(scratch),
        compiler_params=pltpu.CompilerParams(vmem_limit_bytes=limit),
        cost_estimate=pl.CostEstimate(flops=1 << 20, bytes_accessed=1 << 20, transcendentals=0),
    )


def exchanged(value, axes):
    return lax.all_to_all(value, axes, 0, 0, tiled=True)


def swapped(value):
    return lax.ppermute(value, "seq_2", [(0, 1), (1, 0)])


def on_device(
    hidden_in,
    queries,
    key_cache,
    value_cache,
    lengths,
    out_weight,
    norm_gain,
    router,
    expert_ids,
    capacity,
    w_gate,
    w_up,
    w_down,
):
    keep, send, small = call(
        attention_kernel,
        (
            shaped((HALF_ROWS, 128), f32),
            shaped((HALF_ROWS, 128), f32),
            shaped((ROWS, COLS), bf16),
        ),
        (HBM, HBM, HBM, HBM, VMEM, VMEM, VMEM),
        (
            pltpu.SMEM(lengths.shape, jnp.int32),
            pltpu.VMEM(queries.shape, bf16),
            pltpu.VMEM(key_cache.shape, bf16),
            pltpu.VMEM(value_cache.shape, bf16),
            pltpu.VMEM((TOKENS * SUB, 128), f32),
            pltpu.VMEM((2, HALF_ROWS, 128), f32),
            pltpu.SemaphoreType.DMA((3, CHUNKS)),
        ),
        limit=60 << 20,
    )(lengths, queries, key_cache, value_cache, hidden_in, router.T, norm_gain[None, :])
    weight = out_weight.T
    weight_other = swapped(weight)
    got, small = swapped(send), swapped(small)
    partial = call(
        merge_kernel,
        shaped((CHIPS, BLOCK, 128), bf16),
        (VMEM,) * 5,
        (pltpu.VMEM((BLOCK, 128), f32),),
    )(keep, got, weight_other, small, w_gate)
    partial = exchanged(partial, ("seq_0", "seq_1"))
    projected, rest = call(
        project_kernel,
        (shaped((EXPERTS, ROWS, BOTH), bf16), shaped((ROWS, BOTH), f32)),
        (SMEM,) + (VMEM,) * 6,
        (pltpu.VMEM((BLOCK, 128), f32), pltpu.VMEM((ROWS, BOTH), f32)),
    )(expert_ids.T, partial, hidden_in, small, weight, weight_other, w_up)
    projected = exchanged(projected, "exp")
    gained, residual = call(
        gained_kernel,
        (shaped((CHIPS, ROWS, BOTH), bf16), shaped((ROWS, BOTH), f32)),
        (VMEM,) * 6,
        (pltpu.VMEM((ROWS, BOTH), f32),),
    )(projected, rest, norm_gain[None, :], router.T, small, w_down)
    own = exchanged(gained, ("seq_0", "seq_1"))
    other = swapped(own)
    keep, send = call(
        expert_kernel,
        (shaped((CHIPS, 2 * ROWS, COLS), f32), shaped((CHIPS + 1, 2 * ROWS, COLS), bf16)),
        (SMEM,) + (VMEM,) * 6,
        limit=14 << 20,
    )(capacity, own, other, residual, w_gate[0], w_up[0], w_down[0])
    got = swapped(send)
    summed = call(pair_kernel, shaped((CHIPS * EXPERTS, OWNED, COLS), bf16), (VMEM, VMEM))(keep, got)
    summed = exchanged(summed, ("seq_0", "seq_1", "exp"))
    return call(final_kernel, shaped((OWNED, COLS), bf16), (VMEM, VMEM, VMEM))(summed, residual, got)


def solution(mesh):
    split = Mesh(
        mesh.devices.reshape(4, 4, 2, mesh.shape["exp"]), ("seq_0", "seq_1", "seq_2", "exp")
    )
    placed = (
        P("exp", SEQ),
        P(None, "exp"),
        P(None, SEQ, "exp"),
        P(None, SEQ, "exp"),
        P(),
        P("exp", SEQ),
        P(SEQ),
        P(SEQ, None),
        P("exp", None),
        P(),
        P("exp", None, SEQ),
        P("exp", None, SEQ),
        P("exp", SEQ, None),
    )
    return jax.shard_map(
        on_device, mesh=split, in_specs=placed, out_specs=P("exp", SEQ), check_vma=False
    )
```

time: 87.9 us -> 87.2 us (level)
  blocking collectives: 75.4 us -> 70.8 us
  waiting for transfers between devices: 2.74 us -> 4.15 us
  Pallas kernels: 9.12 us -> 10.2 us
    all_to_all x5 -> x4, blocking collectives: 75.4 us -> 70.8 us  [exchanged(): return lax.all_to_all(value, axes, 0, 0, tiled=True)]
    ppermute x2 -> x5, waiting for transfers between devices: 2.74 us -> 4.15 us  [swapped(): return lax.ppermute(value, 'seq_2', [(0, 1), (1, 0)])]
    pallas_call x6, Pallas kernels: 8.94 us -> 10 us  [the longest x1 4.7 us: on_device(): call(attention_kernel, (shaped((HALF_ROWS, 128), f32), shaped((HALF_ROWS,...]
  transfers between devices with their start and end apart: 2 -> 5, of which waited for: 2 -> 3; matrix products, arithmetic and copies ran while one was open for 0% -> 0% of each run, Pallas kernels for 0% -> 5%
where the time goes in v3:
time: 87.2 us; the launch traced here: 87 us
  blocking collectives  70.8 us (81%)
  Pallas kernels  10.2 us (12%)
  waiting for transfers between devices  4.15 us (5%)
    all_to_all x4, blocking collectives, exchanged(): return lax.all_to_all(value, axes, 0, 0, tiled=True)  70.8 us
    pallas_call x1, Pallas kernels, on_device(): call(attention_kernel, (shaped((HALF_ROWS, 128), f32), shaped((HALF_ROWS,...  4.7 us
    ppermute x5, waiting for transfers between devices, swapped(): return lax.ppermute(value, 'seq_2', [(0, 1), (1, 0)])  4.15 us
    pallas_call x1, Pallas kernels, on_device(): call(expert_kernel, (shaped((CHIPS, 2 * ROWS, COLS), f32), shaped((CHIPS...  2.41 us
  transfers between devices with their start and end apart: 5, of which 3 were waited for; matrix products, arithmetic and copies ran while one was open for 0% of the time, Pallas kernels for 5%

profile of v3, /device:TPU:32, one launch (start us, length us, event | category | flops | bytes accessed | tf_op | source)
XLA Modules:
  0.0 87.0 jit_solution(14430475098532698368)
XLA Ops:
  0.0 0.0 collective-permute-start.1
  0.0 4.7 %shard_map.127 = (f32[96,128]{1,0:T(8,128)}, f32[96,128]{1,0:T(8,128)}, bf16[16,192]{1,0:T(8,128)(2,1)}) custom-call(s32[24]{0:T(128)} %lengths_any.1, bf16[24,768]{1,0:T(8,128)(2,1)} %q_any.1, bf16[24,256,128]{2,1,0:T(8,128)(2,1)} %k_any.1, bf16[24,256,128]{2,1,0:T(8,128)(2,1)} %v_any.1, bf16[3,192]{1,0:T(4,128)(2,1)} %hidden_ref.3, ...), custom_call_target="tpu_custom_call" | custom-call | flops 1048576 | bytes 1048576 | tf_op jit(solution)/shard_map/pallas_call | solution.py:373
  4.7 0.0 copy-start.2
  4.7 0.5 collective-permute-start
  5.2 0.1 collective-permute-start.2
  5.3 1.3 %collective-permute-done.2.small_ref = bf16[16,192]{1,0:T(8,128)(2,1)S(1)} collective-permute-done((bf16[16,192]{1,0:T(8,128)(2,1)}, bf16[16,192]{1,0:T(8,128)(2,1)S(1)}, u32[]{:S(2)}, u32[]{:S(2)}) %collective-permute-start.2) | collective-permute-done | bytes 6176 | tf_op jit(solution)/shard_map/ppermute | solution.py:355
  6.6 0.0 collective-permute-done.got_ref
  6.6 0.0 collective-permute-done.1.weight_ref.other_ref
  6.6 0.0 copy-done.1
  6.6 0.0 copy-start.4
  6.6 0.8 copy-done.4
  7.4 0.3 shard_map.128
  7.7 0.0 copy-start
  7.7 0.0 copy-start.5
  7.7 0.0 copy-start.7
  7.7 19.6 %all_to_all.20.in_ref = bf16[16,80,128]{2,1,0:T(8,128)(2,1)S(1)} all-to-all(bf16[16,80,128]{2,1,0:T(8,128)(2,1)S(1)} %shard_map.128), channel_id=1, replica_groups=mesh['seq_0'=4,'seq_1'=4,'seq_2'=2,'exp'=8] {'seq_0','seq_1'}, dimensions={0} | all-to-all | bytes 655360 | tf_op jit(solution)/shard_map/all_to_all | solution.py:351
  27.3 0.0 copy-done.3
  27.4 0.0 copy-done.8
  27.4 0.0 copy-start.9
  27.4 1.5 %shard_map.129 = (bf16[8,16,384]{2,1,0:T(8,128)(2,1)S(1)}, f32[16,384]{1,0:T(8,128)S(1)}) custom-call(s32[2,3]{1,0:T(2,128)S(1)} %bitcast.16, bf16[16,80,128]{2,1,0:T(8,128)(2,1)S(1)} %all_to_all.20.in_ref, bf16[3,192]{1,0:T(4,128)(2,1)S(1)} %copy-done.6, bf16[16,192]{1,0:T(8,128)(2,1)S(1)} %collective-permute-done.2.small_ref, ...), custom_call_target="tpu_custom_call" | custom-call | flops 1048576 | bytes 1048576 | tf_op jit(solution)/shard_map/pallas_call | solution.py:402
  28.9 18.4 %all_to_all.21.in_ref = bf16[8,16,384]{2,1,0:T(8,128)(2,1)S(1)} all-to-all(bf16[8,16,384]{2,1,0:T(8,128)(2,1)S(1)} %get-tuple-element.17), channel_id=1, replica_groups=mesh['seq_0'=4,'seq_1'=4,'seq_2'=2,'exp'=8] {'exp'}, dimensions={0} | all-to-all | bytes 196608 | tf_op jit(solution)/shard_map/all_to_all | solution.py:351
  47.2 0.0 copy-done.5
  47.2 0.4 shard_map.130
  47.7 12.5 %all_to_all.22.own_ref = bf16[16,16,384]{2,1,0:T(8,128)(2,1)S(1)} all-to-all(bf16[16,16,384]{2,1,0:T(8,128)(2,1)S(1)} %get-tuple-element.19), channel_id=1, replica_groups=mesh['seq_0'=4,'seq_1'=4,'seq_2'=2,'exp'=8] {'seq_0','seq_1'}, dimensions={0} | all-to-all | bytes 393216 | tf_op jit(solution)/shard_map/all_to_all | solution.py:351
  60.2 0.0 collective-permute-start.3
  60.2 1.4 %collective-permute-done.3.other_ref = bf16[16,16,384]{2,1,0:T(8,128)(2,1)S(1)} collective-permute-done((bf16[16,16,384]{2,1,0:T(8,128)(2,1)S(1)}, bf16[16,16,384]{2,1,0:T(8,128)(2,1)S(1)}, u32[]{:S(2)}, u32[]{:S(2)}) %collective-permute-start.3) | collective-permute-done | bytes 196640 | tf_op jit(solution)/shard_map/ppermute | solution.py:355
  61.6 2.4 %shard_map.131 = (f32[16,32,192]{2,1,0:T(8,128)S(1)}, bf16[17,32,192]{2,1,0:T(8,128)(2,1)S(1)}) custom-call(s32[8]{0:T(128)S(1)} %copy-done.9, bf16[16,16,384]{2,1,0:T(8,128)(2,1)S(1)} %all_to_all.22.own_ref, bf16[16,16,384]{2,1,0:T(8,128)(2,1)S(1)} %collective-permute-done.3.other_ref, f32[16,384]{1,0:T(8,128)S(1)} %get-tuple-element.20.residual_ref, ...), custom_call_target="tpu_custom_call" | custom-call | flops 1048576 | bytes 1048576 | tf_op jit(solution)/shard_map/pallas_call | solution.py:417
  64.0 0.2 collective-permute-start.4
  64.2 1.4 %collective-permute-done.4.got_ref = bf16[17,32,192]{2,1,0:T(8,128)(2,1)S(1)} collective-permute-done((bf16[17,32,192]{2,1,0:T(8,128)(2,1)S(1)}, bf16[17,32,192]{2,1,0:T(8,128)(2,1)S(1)}, u32[]{:S(2)}, u32[]{:S(2)}) %collective-permute-start.4) | collective-permute-done | bytes 208928 | tf_op jit(solution)/shard_map/ppermute | solution.py:355
  65.7 0.2 shard_map.132
  65.8 20.4 %all_to_all.23.in_ref = bf16[128,3,192]{2,1,0:T(4,128)(2,1)S(1)} all-to-all(bf16[128,3,192]{2,1,0:T(4,128)(2,1)S(1)} %shard_map.132), channel_id=1, replica_groups=mesh['seq_0'=4,'seq_1'=4,'seq_2'=2,'exp'=8] {'seq_0','seq_1','exp'}, dimensions={0} | all-to-all | bytes 294912 | tf_op jit(solution)/shard_map/all_to_all | solution.py:351
  86.2 0.7 shard_map.133
  (9 shorter events, 0.0 us)
Async XLA Ops:
  0.0 6.6 %copy-start.1 = (bf16[1,6144,256]{2,1,0:T(8,128)(2,1)S(1)}, bf16[1,6144,256]{2,1,0:T(8,128)(2,1)}, u32[]{:S(2)}) copy-start(bf16[1,6144,256]{2,1,0:T(8,128)(2,1)} %ahead_ref.3) | copy-start | bytes 9437188
  0.0 6.6 %collective-permute-start.1 = (bf16[192,768]{1,0:T(8,128)(2,1)}, bf16[192,768]{1,0:T(8,128)(2,1)S(1)}, u32[]{:S(2)}, u32[]{:S(2)}) collective-permute-start(bf16[192,768]{1,0:T(8,128)(2,1)} %bitcast.10), channel_id=1, source_target_pairs={{0,8},{8,0},{1,9},{9,1},{2,10},{10,2},{3,11},{11,3},{4,12},{12,4},... | collective-permute-start | bytes 884744 | tf_op jit(solution)/shard_map/ppermute | solution.py:355
  0.0 27.3 %copy-start.3 = (bf16[768,192]{0,1:T(8,128)(2,1)S(1)}, bf16[768,192]{0,1:T(8,128)(2,1)}, u32[]{:S(2)}) copy-start(bf16[768,192]{0,1:T(8,128)(2,1)} %param.18) | copy-start | bytes 884740
  4.7 22.6 %copy-start.2 = (bf16[1,6144,256]{2,1,0:T(8,128)(2,1)S(1)}, bf16[1,6144,256]{2,1,0:T(8,128)(2,1)}, u32[]{:S(2)}) copy-start(bf16[1,6144,256]{2,1,0:T(8,128)(2,1)} %ahead_ref.4) | copy-start | bytes 9437188
  4.7 1.9 %collective-permute-start = (f32[96,128]{1,0:T(8,128)}, f32[96,128]{1,0:T(8,128)S(1)}, u32[]{:S(2)}, u32[]{:S(2)}) collective-permute-start(f32[96,128]{1,0:T(8,128)} %get-tuple-element.15), channel_id=1, source_target_pairs={{0,8},{8,0},{1,9},{9,1},{2,10},{10,2},{3,11},{11,3},{4,12},{12,4},... | collective-permute-start | bytes 147464 | tf_op jit(solution)/shard_map/ppermute | solution.py:355
  5.2 1.4 %collective-permute-start.2 = (bf16[16,192]{1,0:T(8,128)(2,1)}, bf16[16,192]{1,0:T(8,128)(2,1)S(1)}, u32[]{:S(2)}, u32[]{:S(2)}) collective-permute-start(bf16[16,192]{1,0:T(8,128)(2,1)} %get-tuple-element.16), channel_id=1, source_target_pairs={{0,8},{8,0},{1,9},{9,1},{2,10},{10,2},{3,11},{11,3},{4,12},{12,4},... | collective-permute-start | bytes 18440 | tf_op jit(solution)/shard_map/ppermute | solution.py:355
  6.6 0.8 copy-start.4
  7.4 19.9 %copy-start.6 = (bf16[3,192]{1,0:T(4,128)(2,1)S(1)}, bf16[3,192]{1,0:T(4,128)(2,1)}, u32[]{:S(2)}) copy-start(bf16[3,192]{1,0:T(4,128)(2,1)} %hidden_ref.3) | copy-start | bytes 3460
  7.4 19.9 %copy-start.8 = (s32[3,2]{0,1:T(2,128)S(1)}, s32[3,2]{0,1:T(2,128)}, u32[]{:S(2)}) copy-start(s32[3,2]{0,1:T(2,128)} %param.21) | copy-start | bytes 76
  7.7 39.5 %copy-start = (bf16[1,256,6144]{2,1,0:T(8,128)(2,1)S(1)}, bf16[1,256,6144]{2,1,0:T(8,128)(2,1)}, u32[]{:S(2)}) copy-start(bf16[1,256,6144]{2,1,0:T(8,128)(2,1)} %ahead_ref.5) | copy-start | bytes 9437188
  7.7 39.5 %copy-start.5 = (bf16[192,8]{0,1:T(8,128)(2,1)S(1)}, bf16[192,8]{0,1:T(8,128)(2,1)}, u32[]{:S(2)}) copy-start(bf16[192,8]{0,1:T(8,128)(2,1)} %param.20) | copy-start | bytes 9220
  7.7 39.5 %copy-start.7 = (f32[192]{0:T(256)S(1)}, f32[192]{0:T(256)}, u32[]{:S(2)}) copy-start(f32[192]{0:T(256)} %param.19) | copy-start | bytes 2308
  27.4 34.2 %copy-start.9 = (s32[8]{0:T(128)S(1)}, s32[8]{0:T(128)}, u32[]{:S(2)}) copy-start(s32[8]{0:T(128)} %capacity_ref.1) | copy-start | bytes 100
  60.2 1.4 %collective-permute-start.3 = (bf16[16,16,384]{2,1,0:T(8,128)(2,1)S(1)}, bf16[16,16,384]{2,1,0:T(8,128)(2,1)S(1)}, u32[]{:S(2)}, u32[]{:S(2)}) collective-permute-start(bf16[16,16,384]{2,1,0:T(8,128)(2,1)S(1)} %all_to_all.22.own_ref), channel_id=1, source_target_pairs={{0,8},{8,0},{1,9},{9,1},{2,10},{10,2},{3,11},{11,3},{4,12},{12,4},... | collective-permute-start | bytes 589832 | tf_op jit(solution)/shard_map/ppermute | solution.py:355
  64.0 1.6 %collective-permute-start.4 = (bf16[17,32,192]{2,1,0:T(8,128)(2,1)S(1)}, bf16[17,32,192]{2,1,0:T(8,128)(2,1)S(1)}, u32[]{:S(2)}, u32[]{:S(2)}) collective-permute-start(bf16[17,32,192]{2,1,0:T(8,128)(2,1)S(1)} %get-tuple-element.22), channel_id=1, source_target_pairs={{0,8},{8,0},{1,9},{9,1},{2,10},{10,2},{3,11},{11,3},{4,12},{12,4},... | collective-permute-start | bytes 626696 | tf_op jit(solution)/shard_map/ppermute | solution.py:355

commit v4 on v3

--- a/solution.py
+++ b/solution.py
@@ -29,7 +29,6 @@
 bf16 = jnp.bfloat16
 VMEM = pl.BlockSpec(memory_space=pltpu.VMEM)
 SMEM = pl.BlockSpec(memory_space=pltpu.SMEM)
-HBM = pl.BlockSpec(memory_space=pltpu.HBM)
 
 
 def lanes(shape):
@@ -53,54 +52,30 @@
 
 
 def attention_kernel(
-    lengths_any, q_any, k_any, v_any, hidden_ref, router_ref, gain_ref,
-    keep_ref, send_ref, small_ref,
-    lengths_ref, q_ref, kbuf, vbuf, qs, halves, sems,
+    lengths_ref, q_ref, k_ref, v_ref, hidden_ref, router_ref, gain_ref,
+    keep_ref, send_ref, qs, halves,
 ):
-    heads = pltpu.make_async_copy(q_any, q_ref, sems.at[2, 0])
-    limits = pltpu.make_async_copy(lengths_any, lengths_ref, sems.at[2, 1])
-    heads.start()
-    limits.start()
-    copies = []
-    for i in range(CHUNKS):
-        part = pl.ds(i * PER, PER)
-        copies.append(
-            (
-                pltpu.make_async_copy(k_any.at[part], kbuf.at[part], sems.at[0, i]),
-                pltpu.make_async_copy(v_any.at[part], vbuf.at[part], sems.at[1, i]),
-            )
-        )
-    for pair in copies:
-        pair[0].start()
-        pair[1].start()
-    gain = gain_ref[...]
-    gain_hi = rounded(gain)
-    gain_mid = rounded(gain - gain_hi)
-    row = subs((ROWS, COLS))
-    small = jnp.zeros((ROWS, COLS), f32)
-    hidden, router = hidden_ref[...].astype(f32), router_ref[...].astype(f32)
-    lines = [hidden[r : r + 1] for r in range(OWNED)] + [router[r : r + 1] for r in range(EXPERTS)]
-    for r, line in enumerate(lines + [gain_hi, gain_mid, gain - gain_hi - gain_mid]):
-        small = jnp.where(row == r, line, small)
-    small_ref[...] = small.astype(bf16)
+    send_ref[HALF_ROWS:, :] = jnp.zeros((2 * ROWS, 128), f32)
+    first = HALF_ROWS
+    for ref in (hidden_ref, router_ref, gain_ref):
+        lines = ref[...].astype(f32)
+        send_ref[first : first + len(lines), :] = lines[:, :128]
+        send_ref[first + ROWS : first + ROWS + len(lines), : COLS - 128] = lines[:, 128:]
+        first += len(lines)
     qs[...] = jnp.zeros_like(qs)
-    heads.wait()
     for h in range(GROUP):
         qs[pl.ds(h, TOKENS, stride=SUB), :] = q_ref[:, h * HEAD_DIM : (h + 1) * HEAD_DIM].astype(f32)
-    limits.wait()
-    span = k_any.shape[1]
+    span = k_ref.shape[1]
     first = lax.axis_index(SEQ) * span
     places = first + lanes((SUB, span))
     lane, sub = lanes((SUB, 128)), subs((SUB, 128))
     scale = 1.0 / math.sqrt(HEAD_DIM)
     for i in range(CHUNKS):
-        copies[i][0].wait()
         scores = []
         for b in range(i * PER, (i + 1) * PER):
             query = qs[b * SUB : (b + 1) * SUB, :].astype(bf16)
-            s = lax.dot_general(query, kbuf[b], (((1,), (1,)), ((), ())), preferred_element_type=f32)
+            s = lax.dot_general(query, k_ref[b], (((1,), (1,)), ((), ())), preferred_element_type=f32)
             scores.append(jnp.where(places < lengths_ref[b], s * scale, masked_score))
-        copies[i][1].wait()
         for n, b in enumerate(range(i * PER, (i + 1) * PER)):
             s = scores[n]
             peak = rounded(jnp.max(s, axis=-1, keepdims=True))
@@ -108,7 +83,7 @@
             total = jnp.sum(p, axis=-1, keepdims=True)
             p_hi = rounded(p)
             both = jnp.concatenate([p_hi, p - p_hi], axis=0).astype(bf16)
-            weighted = jnp.dot(both, vbuf[b], preferred_element_type=f32)
+            weighted = jnp.dot(both, v_ref[b], preferred_element_type=f32)
             weighted = weighted[:SUB] + weighted[SUB:]
             stats = jnp.where(lane == sub, peak, 0.0)
             stats = jnp.where(lane == sub + SUB, total, stats)
@@ -117,7 +92,7 @@
             halves[half, line : line + SUB, :] = jnp.where(sub == GROUP, stats, weighted)
     core = lax.axis_index("seq_2")
     keep_ref[...] = halves[core]
-    send_ref[...] = halves[1 - core]
+    send_ref[:HALF_ROWS, :] = halves[1 - core]
 
 
 def as_column(x):
@@ -126,10 +101,10 @@
     return jnp.sum(jnp.where(lanes(shape) == subs(shape), wide, 0.0), axis=2, keepdims=True)
 
 
-def merge_kernel(keep_ref, got_ref, weight_ref, small_ref, ahead_ref, out_ref, packed):
+def merge_kernel(keep_ref, got_ref, weight_ref, ahead_ref, out_ref, packed):
     shape = (HALF, SUB, 128)
     sub = subs(shape)
-    blocks = [ref[...].reshape(shape) for ref in (keep_ref, got_ref)]
+    blocks = [ref[:HALF_ROWS, :].reshape(shape) for ref in (keep_ref, got_ref)]
     stats = [jnp.sum(jnp.where(sub == GROUP, x, 0.0), axis=1, keepdims=True) for x in blocks]
     peak = jnp.maximum(stats[0], stats[1])
     weighted, total = jnp.zeros(shape, f32), jnp.zeros((HALF, 1, 128), f32)
@@ -154,8 +129,14 @@
         out_ref[i] = block
 
 
+def others(ref, first, count):
+    line = HALF_ROWS + first
+    left = ref[line : line + count, :]
+    return jnp.concatenate([left, ref[line + ROWS : line + ROWS + count, : COLS - 128]], axis=1)
+
+
 def project_kernel(
-    ids_ref, in_ref, hidden_ref, small_ref, weight_ref, other_ref, ahead_ref, out_ref, rest_ref, att, wide
+    ids_ref, in_ref, hidden_ref, got_ref, weight_ref, other_ref, ahead_ref, out_ref, rest_ref, att, wide
 ):
     core, me = lax.axis_index("seq_2"), lax.axis_index("exp")
     tiles = [in_ref[i, PACKED:, :].astype(f32) for i in range(CHIPS)]
@@ -189,7 +170,7 @@
         acc_other += lax.dot_general(rows, other_ref[:, cols], over_features, preferred_element_type=f32)
     mine = OWNED * me - HALF * core
     row = subs((HALF, COLS))
-    hidden, hidden_other = hidden_ref[...].astype(f32), small_ref[...].astype(f32)
+    hidden, hidden_other = hidden_ref[...].astype(f32), others(got_ref, 0, OWNED)
     for r in range(OWNED):
         acc += jnp.where(row == mine + r, hidden[r : r + 1, :], 0.0)
         acc_other += jnp.where(row == mine + r, hidden_other[r : r + 1, :], 0.0)
@@ -210,16 +191,14 @@
     rest_ref[...] = jnp.where(owned, full - sent.astype(f32), 0.0)
 
 
-def gained_kernel(in_ref, rest_ref, gain_ref, router_ref, small_ref, ahead_ref, out_ref, residual_ref, wide):
+def gained_kernel(in_ref, rest_ref, gain_ref, router_ref, got_ref, ahead_ref, out_ref, residual_ref, wide):
     core = lax.axis_index("seq_2")
     total = rest_ref[...]
     for i in range(EXPERTS):
         total += in_ref[i].astype(f32)
     residual_ref[...] = total
-    small = small_ref[...].astype(f32)
-    router, router_other = router_ref[...].astype(f32), small[OWNED : OWNED + EXPERTS]
-    gain = gain_ref[...]
-    gain_other = small[11:12] + (small[12:13] + small[13:14])
+    router, router_other = router_ref[...].astype(f32), others(got_ref, OWNED, EXPERTS)
+    gain, gain_other = gain_ref[...], others(got_ref, OWNED + EXPERTS, 1)
     wide[:EXPERTS, :COLS] = jnp.where(core == 0, router, router_other)
     wide[:EXPERTS, COLS:] = jnp.where(core == 0, router_other, router)
     wide[EXPERTS : EXPERTS + 1, :COLS] = jnp.where(core == 0, gain, gain_other)
@@ -315,7 +294,10 @@
         total = keep_ref[k] + got_ref[k].astype(f32)
         for e in range(EXPERTS):
             line = ROWS * (e // 4) + OWNED * (e % 4)
-            out_ref[EXPERTS * k + e] = total[line : line + OWNED, :].astype(bf16)
+            out_ref[EXPERTS * k + e, :, :COLS] = total[line : line + 2, :].astype(bf16)
+            last = total[line + 2 : line + OWNED, :]
+            last = jnp.concatenate([last[:, : COLS // 2], last[:, COLS // 2 :]], axis=0)
+            out_ref[EXPERTS * k + e, :, COLS:] = last.astype(bf16)
 
 
 def final_kernel(in_ref, residual_ref, got_ref, out_ref):
@@ -327,7 +309,9 @@
     total = jnp.zeros((OWNED, COLS), f32)
     for q in range(4):
         total += jnp.where(me % 4 == q, residual[OWNED * q : OWNED * (q + 1), :], 0.0)
-    out_ref[...] = (total + jnp.sum(in_ref[...].astype(f32), axis=0)).astype(bf16)
+    experts = jnp.sum(in_ref[...].astype(f32), axis=0)
+    last = jnp.concatenate([experts[:1, COLS:], experts[1:, COLS:]], axis=1)
+    out_ref[...] = (total + jnp.concatenate([experts[:, :COLS], last], axis=0)).astype(bf16)
 
 
 def shaped(shape, dtype):
@@ -345,6 +329,10 @@
         compiler_params=pltpu.CompilerParams(vmem_limit_bytes=limit),
         cost_estimate=pl.CostEstimate(flops=1 << 20, bytes_accessed=1 << 20, transcendentals=0),
     )
+
+
+def in_hbm(x):
+    return pltpu.with_memory_space_constraint(x, pltpu.HBM)
 
 
 def exchanged(value, axes):
@@ -370,48 +358,42 @@
     w_up,
     w_down,
 ):
-    keep, send, small = call(
+    keep, send = call(
         attention_kernel,
         (
             shaped((HALF_ROWS, 128), f32),
-            shaped((HALF_ROWS, 128), f32),
-            shaped((ROWS, COLS), bf16),
+            shaped((HALF_ROWS + 2 * ROWS, 128), f32),
         ),
-        (HBM, HBM, HBM, HBM, VMEM, VMEM, VMEM),
+        (SMEM,) + (VMEM,) * 6,
         (
-            pltpu.SMEM(lengths.shape, jnp.int32),
-            pltpu.VMEM(queries.shape, bf16),
-            pltpu.VMEM(key_cache.shape, bf16),
-            pltpu.VMEM(value_cache.shape, bf16),
             pltpu.VMEM((TOKENS * SUB, 128), f32),
             pltpu.VMEM((2, HALF_ROWS, 128), f32),
-            pltpu.SemaphoreType.DMA((3, CHUNKS)),
         ),
-        limit=60 << 20,
-    )(lengths, queries, key_cache, value_cache, hidden_in, router.T, norm_gain[None, :])
+        limit=8 << 20,
+    )(*(in_hbm(x) for x in (lengths, queries, key_cache, value_cache, hidden_in, router.T, norm_gain[None, :])))
     weight = out_weight.T
     weight_other = swapped(weight)
-    got, small = swapped(send), swapped(small)
+    got_partial = swapped(send)
     partial = call(
         merge_kernel,
         shaped((CHIPS, BLOCK, 128), bf16),
-        (VMEM,) * 5,
+        (VMEM,) * 4,
         (pltpu.VMEM((BLOCK, 128), f32),),
-    )(keep, got, weight_other, small, w_gate)
+    )(keep, got_partial, weight_other, w_gate)
     partial = exchanged(partial, ("seq_0", "seq_1"))
     projected, rest = call(
         project_kernel,
         (shaped((EXPERTS, ROWS, BOTH), bf16), shaped((ROWS, BOTH), f32)),
         (SMEM,) + (VMEM,) * 6,
         (pltpu.VMEM((BLOCK, 128), f32), pltpu.VMEM((ROWS, BOTH), f32)),
-    )(expert_ids.T, partial, hidden_in, small, weight, weight_other, w_up)
+    )(expert_ids.T, partial, hidden_in, got_partial, weight, weight_other, w_up)
     projected = exchanged(projected, "exp")
     gained, residual = call(
         gained_kernel,
         (shaped((CHIPS, ROWS, BOTH), bf16), shaped((ROWS, BOTH), f32)),
         (VMEM,) * 6,
         (pltpu.VMEM((ROWS, BOTH), f32),),
-    )(projected, rest, norm_gain[None, :], router.T, small, w_down)
+    )(projected, rest, norm_gain[None, :], router.T, got_partial, w_down)
     own = exchanged(gained, ("seq_0", "seq_1"))
     other = swapped(own)
     keep, send = call(
@@ -421,7 +403,7 @@
         limit=14 << 20,
     )(capacity, own, other, residual, w_gate[0], w_up[0], w_down[0])
     got = swapped(send)
-    summed = call(pair_kernel, shaped((CHIPS * EXPERTS, OWNED, COLS), bf16), (VMEM, VMEM))(keep, got)
+    summed = call(pair_kernel, shaped((CHIPS * EXPERTS, 2, COLS + COLS // 2), bf16), (VMEM, VMEM))(keep, got)
     summed = exchanged(summed, ("seq_0", "seq_1", "exp"))
     return call(final_kernel, shaped((OWNED, COLS), bf16), (VMEM, VMEM, VMEM))(summed, residual, got)
 

time: 87.2 us -> 84.1 us (0.964)
  blocking collectives: 70.8 us -> 69.7 us
    all_to_all x4, blocking collectives: 70.8 us -> 69.7 us  [exchanged(): return lax.all_to_all(value, axes, 0, 0, tiled=True)]
    pallas_call x3, Pallas kernels: 5.15 us -> 4.18 us  [the longest x1 3.44 us: on_device(): call(attention_kernel, (shaped((HALF_ROWS, 128), f32), shaped((HALF_ROWS...]
    ppermute x5 -> x4, waiting for transfers between devices: 4.15 us -> 3.76 us  [swapped(): return lax.ppermute(value, 'seq_2', [(0, 1), (1, 0)])]
  transfers between devices with their start and end apart: 5 -> 4, of which waited for: 3 -> 3; matrix products, arithmetic and copies ran while one was open for 0% -> 0% of each run, Pallas kernels for 5% -> 4%
where the time goes in v4:
time: 84.1 us; the launch traced here: 83.9 us
  blocking collectives  69.7 us (83%)
  Pallas kernels  9.39 us (11%)
  waiting for transfers between devices  3.76 us (4%)
  starting transfers between devices  0.91 us (1%)
    all_to_all x4, blocking collectives, exchanged(): return lax.all_to_all(value, axes, 0, 0, tiled=True)  69.7 us
    ppermute x4, waiting for transfers between devices, swapped(): return lax.ppermute(value, 'seq_2', [(0, 1), (1, 0)])  3.76 us
    pallas_call x1, Pallas kernels, on_device(): call(attention_kernel, (shaped((HALF_ROWS, 128), f32), shaped((HALF_ROWS...  3.44 us
    pallas_call x1, Pallas kernels, on_device(): call(expert_kernel, (shaped((CHIPS, 2 * ROWS, COLS), f32), shaped((CHIPS...  2.41 us
  transfers between devices with their start and end apart: 4, of which 3 were waited for; matrix products, arithmetic and copies ran while one was open for 0% of the time, Pallas kernels for 4%

profile of v4, /device:TPU:32, one launch (start us, length us, event | category | flops | bytes accessed | tf_op | source)
XLA Modules:
  0.0 83.9 jit_solution(2265393047171858859)
XLA Ops:
  0.0 0.0 collective-permute-start.1
  0.0 0.0 copy-start.3
  0.0 0.0 copy-start.5
  0.0 0.0 copy-start.7
  0.0 3.4 %shard_map.127 = (f32[96,128]{1,0:T(8,128)S(1)}, f32[128,128]{1,0:T(8,128)S(1)}) custom-call(s32[24]{0:T(128)} %lengths_ref.1, bf16[24,768]{1,0:T(8,128)(2,1)} %q_ref.1, bf16[24,256,128]{2,1,0:T(8,128)(2,1)} %k_ref.1, bf16[24,256,128]{2,1,0:T(8,128)(2,1)} %v_ref.1, bf16[3,192]{1,0:T(4,128)(2,1)} %hidden_ref.3, bf16[8,192]{1,0:T(8,128)(2,1)} %bitcast.12, ...), custom_call_target="tpu_custom_call" | custom-call | flops 1048576 | bytes 1048576 | tf_op jit(solution)/shard_map/pallas_call | solution.py:361
  3.5 0.7 collective-permute-start
  4.2 0.9 %collective-permute-done.got_ref = f32[128,128]{1,0:T(8,128)S(1)} collective-permute-done((f32[128,128]{1,0:T(8,128)S(1)}, f32[128,128]{1,0:T(8,128)S(1)}, u32[]{:S(2)}, u32[]{:S(2)}) %collective-permute-start) | collective-permute-done | bytes 65568 | tf_op jit(solution)/shard_map/ppermute | solution.py:343
  5.1 0.0 collective-permute-done.1.weight_ref.other_ref
  5.1 0.0 copy-done.1
  5.1 0.3 shard_map.128
  5.4 0.0 copy-start
  5.4 0.0 copy-start.4
  5.4 0.0 copy-start.6
  5.4 19.8 %all_to_all.20.in_ref = bf16[16,80,128]{2,1,0:T(8,128)(2,1)S(1)} all-to-all(bf16[16,80,128]{2,1,0:T(8,128)(2,1)S(1)} %shard_map.128), channel_id=1, replica_groups=mesh['seq_0'=4,'seq_1'=4,'seq_2'=2,'exp'=8] {'seq_0','seq_1'}, dimensions={0} | all-to-all | bytes 655360 | tf_op jit(solution)/shard_map/all_to_all | solution.py:339
  25.2 0.0 copy-done.2
  25.2 0.0 copy-done.3
  25.2 0.0 copy-done.5
  25.2 0.0 copy-done.7
  25.2 0.0 copy-start.8
  25.2 1.5 %shard_map.129 = (bf16[8,16,384]{2,1,0:T(8,128)(2,1)S(1)}, f32[16,384]{1,0:T(8,128)S(1)}) custom-call(s32[2,3]{1,0:T(2,128)S(1)} %bitcast.16, bf16[16,80,128]{2,1,0:T(8,128)(2,1)S(1)} %all_to_all.20.in_ref, bf16[3,192]{1,0:T(4,128)(2,1)S(1)} %copy-done.5, f32[128,128]{1,0:T(8,128)S(1)} %collective-permute-done.got_ref, bf16[192,768]{1,0:T(8,128)(2,1)S(1)} %bitcast.11, ...), custom_call_target="tpu_custom_call" | custom-call | flops 1048576 | bytes 1048576 | tf_op jit(solution)/shard_map/pallas_call | solution.py:384
  26.7 18.4 %all_to_all.21.in_ref = bf16[8,16,384]{2,1,0:T(8,128)(2,1)S(1)} all-to-all(bf16[8,16,384]{2,1,0:T(8,128)(2,1)S(1)} %get-tuple-element.15), channel_id=1, replica_groups=mesh['seq_0'=4,'seq_1'=4,'seq_2'=2,'exp'=8] {'exp'}, dimensions={0} | all-to-all | bytes 196608 | tf_op jit(solution)/shard_map/all_to_all | solution.py:339
  45.1 0.0 copy-done.6
  45.1 0.4 shard_map.130
  45.5 12.5 %all_to_all.22.own_ref = bf16[16,16,384]{2,1,0:T(8,128)(2,1)S(1)} all-to-all(bf16[16,16,384]{2,1,0:T(8,128)(2,1)S(1)} %get-tuple-element.17), channel_id=1, replica_groups=mesh['seq_0'=4,'seq_1'=4,'seq_2'=2,'exp'=8] {'seq_0','seq_1'}, dimensions={0} | all-to-all | bytes 393216 | tf_op jit(solution)/shard_map/all_to_all | solution.py:339
  58.0 0.0 collective-permute-start.2
  58.0 1.4 %collective-permute-done.2.other_ref = bf16[16,16,384]{2,1,0:T(8,128)(2,1)S(1)} collective-permute-done((bf16[16,16,384]{2,1,0:T(8,128)(2,1)S(1)}, bf16[16,16,384]{2,1,0:T(8,128)(2,1)S(1)}, u32[]{:S(2)}, u32[]{:S(2)}) %collective-permute-start.2) | collective-permute-done | bytes 196640 | tf_op jit(solution)/shard_map/ppermute | solution.py:343
  59.4 2.4 %shard_map.131 = (f32[16,32,192]{2,1,0:T(8,128)S(1)}, bf16[17,32,192]{2,1,0:T(8,128)(2,1)S(1)}) custom-call(s32[8]{0:T(128)S(1)} %copy-done.8, bf16[16,16,384]{2,1,0:T(8,128)(2,1)S(1)} %all_to_all.22.own_ref, bf16[16,16,384]{2,1,0:T(8,128)(2,1)S(1)} %collective-permute-done.2.other_ref, f32[16,384]{1,0:T(8,128)S(1)} %get-tuple-element.18.residual_ref, ...), custom_call_target="tpu_custom_call" | custom-call | flops 1048576 | bytes 1048576 | tf_op jit(solution)/shard_map/pallas_call | solution.py:399
  61.9 0.2 collective-permute-start.3
  62.1 1.4 %collective-permute-done.3.got_ref = bf16[17,32,192]{2,1,0:T(8,128)(2,1)S(1)} collective-permute-done((bf16[17,32,192]{2,1,0:T(8,128)(2,1)S(1)}, bf16[17,32,192]{2,1,0:T(8,128)(2,1)S(1)}, u32[]{:S(2)}, u32[]{:S(2)}) %collective-permute-start.3) | collective-permute-done | bytes 208928 | tf_op jit(solution)/shard_map/ppermute | solution.py:343
  63.5 0.5 shard_map.132
  64.0 19.1 %all_to_all.23.in_ref = bf16[128,2,288]{2,1,0:T(2,128)(2,1)S(1)} all-to-all(bf16[128,2,288]{2,1,0:T(2,128)(2,1)S(1)} %shard_map.132), channel_id=1, replica_groups=mesh['seq_0'=4,'seq_1'=4,'seq_2'=2,'exp'=8] {'seq_0','seq_1','exp'}, dimensions={0} | all-to-all | bytes 294912 | tf_op jit(solution)/shard_map/all_to_all | solution.py:339
  83.1 0.9 %shard_map.133 = bf16[3,192]{1,0:T(4,128)(2,1)} custom-call(bf16[128,2,288]{2,1,0:T(2,128)(2,1)S(1)} %all_to_all.23.in_ref, f32[16,384]{1,0:T(8,128)S(1)} %get-tuple-element.18.residual_ref, bf16[17,32,192]{2,1,0:T(8,128)(2,1)S(1)} %collective-permute-done.3.got_ref), custom_call_target="tpu_custom_call" | custom-call | flops 1048576 | bytes 1048576 | tf_op jit(solution)/shard_map/pallas_call | solution.py:408
  (5 shorter events, 0.0 us)
Async XLA Ops:
  0.0 5.1 %copy-start.1 = (bf16[1,6144,256]{2,1,0:T(8,128)(2,1)S(1)}, bf16[1,6144,256]{2,1,0:T(8,128)(2,1)}, u32[]{:S(2)}) copy-start(bf16[1,6144,256]{2,1,0:T(8,128)(2,1)} %ahead_ref.3) | copy-start | bytes 9437188
  0.0 5.1 %collective-permute-start.1 = (bf16[192,768]{1,0:T(8,128)(2,1)}, bf16[192,768]{1,0:T(8,128)(2,1)S(1)}, u32[]{:S(2)}, u32[]{:S(2)}) collective-permute-start(bf16[192,768]{1,0:T(8,128)(2,1)} %bitcast.10), channel_id=1, source_target_pairs={{0,8},{8,0},{1,9},{9,1},{2,10},{10,2},{3,11},{11,3},{4,12},{12,4},... | collective-permute-start | bytes 884744 | tf_op jit(solution)/shard_map/ppermute | solution.py:343
  0.0 25.2 %copy-start.2 = (bf16[1,6144,256]{2,1,0:T(8,128)(2,1)S(1)}, bf16[1,6144,256]{2,1,0:T(8,128)(2,1)}, u32[]{:S(2)}) copy-start(bf16[1,6144,256]{2,1,0:T(8,128)(2,1)} %ahead_ref.4) | copy-start | bytes 9437188
  0.0 25.2 %copy-start.3 = (bf16[768,192]{0,1:T(8,128)(2,1)S(1)}, bf16[768,192]{0,1:T(8,128)(2,1)}, u32[]{:S(2)}) copy-start(bf16[768,192]{0,1:T(8,128)(2,1)} %param.18) | copy-start | bytes 884740
  0.0 25.2 %copy-start.5 = (bf16[3,192]{1,0:T(4,128)(2,1)S(1)}, bf16[3,192]{1,0:T(4,128)(2,1)}, u32[]{:S(2)}) copy-start(bf16[3,192]{1,0:T(4,128)(2,1)} %hidden_ref.3) | copy-start | bytes 3460
  0.0 25.2 %copy-start.7 = (s32[3,2]{0,1:T(2,128)S(1)}, s32[3,2]{0,1:T(2,128)}, u32[]{:S(2)}) copy-start(s32[3,2]{0,1:T(2,128)} %param.21) | copy-start | bytes 76
  3.5 1.6 %collective-permute-start = (f32[128,128]{1,0:T(8,128)S(1)}, f32[128,128]{1,0:T(8,128)S(1)}, u32[]{:S(2)}, u32[]{:S(2)}) collective-permute-start(f32[128,128]{1,0:T(8,128)S(1)} %get-tuple-element.14), channel_id=1, source_target_pairs={{0,8},{8,0},{1,9},{9,1},{2,10},{10,2},{3,11},{11,3},{4,12},{12,4},... | collective-permute-start | bytes 196616 | tf_op jit(solution)/shard_map/ppermute | solution.py:343
  5.4 39.7 %copy-start = (bf16[1,256,6144]{2,1,0:T(8,128)(2,1)S(1)}, bf16[1,256,6144]{2,1,0:T(8,128)(2,1)}, u32[]{:S(2)}) copy-start(bf16[1,256,6144]{2,1,0:T(8,128)(2,1)} %ahead_ref.5) | copy-start | bytes 9437188
  5.4 39.7 %copy-start.4 = (bf16[192,8]{0,1:T(8,128)(2,1)S(1)}, bf16[192,8]{0,1:T(8,128)(2,1)}, u32[]{:S(2)}) copy-start(bf16[192,8]{0,1:T(8,128)(2,1)} %param.20) | copy-start | bytes 9220
  5.4 39.7 %copy-start.6 = (f32[192]{0:T(256)S(1)}, f32[192]{0:T(256)}, u32[]{:S(2)}) copy-start(f32[192]{0:T(256)} %param.19) | copy-start | bytes 2308
  25.2 34.2 %copy-start.8 = (s32[8]{0:T(128)S(1)}, s32[8]{0:T(128)}, u32[]{:S(2)}) copy-start(s32[8]{0:T(128)} %capacity_ref.1) | copy-start | bytes 100
  58.0 1.4 %collective-permute-start.2 = (bf16[16,16,384]{2,1,0:T(8,128)(2,1)S(1)}, bf16[16,16,384]{2,1,0:T(8,128)(2,1)S(1)}, u32[]{:S(2)}, u32[]{:S(2)}) collective-permute-start(bf16[16,16,384]{2,1,0:T(8,128)(2,1)S(1)} %all_to_all.22.own_ref), channel_id=1, source_target_pairs={{0,8},{8,0},{1,9},{9,1},{2,10},{10,2},{3,11},{11,3},{4,12},{12,4},... | collective-permute-start | bytes 589832 | tf_op jit(solution)/shard_map/ppermute | solution.py:343
  61.9 1.6 %collective-permute-start.3 = (bf16[17,32,192]{2,1,0:T(8,128)(2,1)S(1)}, bf16[17,32,192]{2,1,0:T(8,128)(2,1)S(1)}, u32[]{:S(2)}, u32[]{:S(2)}) collective-permute-start(bf16[17,32,192]{2,1,0:T(8,128)(2,1)S(1)} %get-tuple-element.20), channel_id=1, source_target_pairs={{0,8},{8,0},{1,9},{9,1},{2,10},{10,2},{3,11},{11,3},{4,12},{12,4},... | collective-permute-start | bytes 626696 | tf_op jit(solution)/shard_map/ppermute | solution.py:343

commit v5 on v4

--- a/solution.py
+++ b/solution.py
@@ -175,11 +175,11 @@
         acc += jnp.where(row == mine + r, hidden[r : r + 1, :], 0.0)
         acc_other += jnp.where(row == mine + r, hidden_other[r : r + 1, :], 0.0)
     row, lane = subs((ROWS, BOTH)), lanes((ROWS, BOTH))
-    ids = jnp.zeros((ROWS, BOTH), f32)
+    ids, given = jnp.zeros((ROWS, BOTH), f32), ids_ref[...].astype(f32)
     for r in range(OWNED):
         for k in range(2):
             here = (row == HALF) & (lane == 2 * (OWNED * me + r) + k)
-            ids = jnp.where(here, ids_ref[k, r].astype(f32), ids)
+            ids = jnp.where(here, given[k : k + 1, r : r + 1], ids)
     wide[...] = ids
     wide[:HALF, :COLS] = jnp.where(core == 0, acc, acc_other)
     wide[:HALF, COLS:] = jnp.where(core == 0, acc_other, acc)
@@ -273,7 +273,9 @@
     place = inside % OWNED
     earlier = jnp.where(place >= 1, pltpu.roll(naming, 1, 0), 0.0)
     earlier += jnp.where(place >= 2, pltpu.roll(naming, 2, 0), 0.0)
-    kept = names & (earlier[:, :1] < capacity_ref[me].astype(f32)) & (inside[:, :1] < HALF)
+    limits = capacity_ref[...].astype(f32)
+    limit = jnp.sum(jnp.where(lanes((1, EXPERTS)) == me, limits, 0.0), axis=-1, keepdims=True)
+    kept = names & (earlier[:, :1] < limit) & (inside[:, :1] < HALF)
     weight = jnp.where(kept, routed, 0.0)
     gate, up = gate * scale, up * scale
     inner = (gate / (1.0 + jnp.exp(-gate)) * up * weight).astype(bf16)
@@ -290,14 +292,16 @@
 
 
 def pair_kernel(keep_ref, got_ref, out_ref):
+    first = subs((2 * ROWS, COLS // 2)) % ROWS % OWNED == 0
     for k in range(CHIPS):
         total = keep_ref[k] + got_ref[k].astype(f32)
+        left, right = total[:, : COLS // 2], total[:, COLS // 2 :]
+        left = jnp.concatenate([left[2:], left[:2]], axis=0)
+        right = jnp.concatenate([right[1:], right[:1]], axis=0)
+        wide = jnp.concatenate([total, jnp.where(first, left, right)], axis=1)
         for e in range(EXPERTS):
             line = ROWS * (e // 4) + OWNED * (e % 4)
-            out_ref[EXPERTS * k + e, :, :COLS] = total[line : line + 2, :].astype(bf16)
-            last = total[line + 2 : line + OWNED, :]
-            last = jnp.concatenate([last[:, : COLS // 2], last[:, COLS // 2 :]], axis=0)
-            out_ref[EXPERTS * k + e, :, COLS:] = last.astype(bf16)
+            out_ref[EXPERTS * k + e] = wide[line : line + 2, :].astype(bf16)
 
 
 def final_kernel(in_ref, residual_ref, got_ref, out_ref):
@@ -384,7 +388,7 @@
     projected, rest = call(
         project_kernel,
         (shaped((EXPERTS, ROWS, BOTH), bf16), shaped((ROWS, BOTH), f32)),
-        (SMEM,) + (VMEM,) * 6,
+        (VMEM,) * 7,
         (pltpu.VMEM((BLOCK, 128), f32), pltpu.VMEM((ROWS, BOTH), f32)),
     )(expert_ids.T, partial, hidden_in, got_partial, weight, weight_other, w_up)
     projected = exchanged(projected, "exp")
@@ -399,9 +403,9 @@
     keep, send = call(
         expert_kernel,
         (shaped((CHIPS, 2 * ROWS, COLS), f32), shaped((CHIPS + 1, 2 * ROWS, COLS), bf16)),
-        (SMEM,) + (VMEM,) * 6,
+        (VMEM,) * 7,
         limit=14 << 20,
-    )(capacity, own, other, residual, w_gate[0], w_up[0], w_down[0])
+    )(capacity[None, :], own, other, residual, w_gate[0], w_up[0], w_down[0])
     got = swapped(send)
     summed = call(pair_kernel, shaped((CHIPS * EXPERTS, 2, COLS + COLS // 2), bf16), (VMEM, VMEM))(keep, got)
     summed = exchanged(summed, ("seq_0", "seq_1", "exp"))

time: 84.1 us -> 83 us (0.987)
  Pallas kernels: 9.39 us -> 8.21 us
where the time goes in v5:
time: 83 us; the launch traced here: 82.7 us
  blocking collectives  69.7 us (84%)
  Pallas kernels  8.21 us (10%)
  waiting for transfers between devices  3.76 us (5%)
  starting transfers between devices  0.91 us (1%)
    all_to_all x4, blocking collectives, exchanged(): return lax.all_to_all(value, axes, 0, 0, tiled=True)  69.7 us
    ppermute x4, waiting for transfers between devices, swapped(): return lax.ppermute(value, 'seq_2', [(0, 1), (1, 0)])  3.76 us
    pallas_call x1, Pallas kernels, on_device(): call(attention_kernel, (shaped((HALF_ROWS, 128), f32), shaped((HALF_ROWS...  3.44 us
    pallas_call x1, Pallas kernels, on_device(): call(expert_kernel, (shaped((CHIPS, 2 * ROWS, COLS), f32), shaped((CHIPS...  1.87 us
  transfers between devices with their start and end apart: 4, of which 3 were waited for; matrix products, arithmetic and copies ran while one was open for 0% of the time, Pallas kernels for 4%

profile of v5, /device:TPU:32, one launch (start us, length us, event | category | flops | bytes accessed | tf_op | source)
XLA Modules:
  0.0 82.7 jit_solution(8565366149283377927)
XLA Ops:
  0.0 0.0 collective-permute-start.1
  0.0 0.0 copy-start.3
  0.0 0.0 copy-start.5
  0.0 0.0 copy-start.7
  0.0 3.4 %shard_map.127 = (f32[96,128]{1,0:T(8,128)S(1)}, f32[128,128]{1,0:T(8,128)S(1)}) custom-call(s32[24]{0:T(128)} %lengths_ref.1, bf16[24,768]{1,0:T(8,128)(2,1)} %q_ref.1, bf16[24,256,128]{2,1,0:T(8,128)(2,1)} %k_ref.1, bf16[24,256,128]{2,1,0:T(8,128)(2,1)} %v_ref.1, bf16[3,192]{1,0:T(4,128)(2,1)} %hidden_ref.3, bf16[8,192]{1,0:T(8,128)(2,1)} %bitcast.13, ...), custom_call_target="tpu_custom_call" | custom-call | flops 1048576 | bytes 1048576 | tf_op jit(solution)/shard_map/pallas_call | solution.py:365
  3.5 0.7 collective-permute-start
  4.2 0.9 %collective-permute-done.got_ref = f32[128,128]{1,0:T(8,128)S(1)} collective-permute-done((f32[128,128]{1,0:T(8,128)S(1)}, f32[128,128]{1,0:T(8,128)S(1)}, u32[]{:S(2)}, u32[]{:S(2)}) %collective-permute-start) | collective-permute-done | bytes 65568 | tf_op jit(solution)/shard_map/ppermute | solution.py:347
  5.1 0.0 collective-permute-done.1.weight_ref.other_ref
  5.1 0.0 copy-done.1
  5.1 0.3 shard_map.128
  5.4 0.0 copy-start
  5.4 0.0 copy-start.4
  5.4 0.0 copy-start.6
  5.4 19.8 %all_to_all.20.in_ref = bf16[16,80,128]{2,1,0:T(8,128)(2,1)S(1)} all-to-all(bf16[16,80,128]{2,1,0:T(8,128)(2,1)S(1)} %shard_map.128), channel_id=1, replica_groups=mesh['seq_0'=4,'seq_1'=4,'seq_2'=2,'exp'=8] {'seq_0','seq_1'}, dimensions={0} | all-to-all | bytes 655360 | tf_op jit(solution)/shard_map/all_to_all | solution.py:343
  25.2 0.0 copy-done.2
  25.2 0.0 copy-done.3
  25.2 0.0 copy-done.5
  25.2 0.0 copy-done.7
  25.2 0.0 copy-start.8
  25.2 1.0 %shard_map.129 = (bf16[8,16,384]{2,1,0:T(8,128)(2,1)S(1)}, f32[16,384]{1,0:T(8,128)S(1)}) custom-call(s32[2,3]{1,0:T(2,128)S(1)} %bitcast.17, bf16[16,80,128]{2,1,0:T(8,128)(2,1)S(1)} %all_to_all.20.in_ref, bf16[3,192]{1,0:T(4,128)(2,1)S(1)} %copy-done.5, f32[128,128]{1,0:T(8,128)S(1)} %collective-permute-done.got_ref, bf16[192,768]{1,0:T(8,128)(2,1)S(1)} %bitcast.12, ...), custom_call_target="tpu_custom_call" | custom-call | flops 1048576 | bytes 1048576 | tf_op jit(solution)/shard_map/pallas_call | solution.py:388
  26.2 18.4 %all_to_all.21.in_ref = bf16[8,16,384]{2,1,0:T(8,128)(2,1)S(1)} all-to-all(bf16[8,16,384]{2,1,0:T(8,128)(2,1)S(1)} %get-tuple-element.15), channel_id=1, replica_groups=mesh['seq_0'=4,'seq_1'=4,'seq_2'=2,'exp'=8] {'exp'}, dimensions={0} | all-to-all | bytes 196608 | tf_op jit(solution)/shard_map/all_to_all | solution.py:343
  44.5 0.0 copy-done
  44.5 0.4 shard_map.130
  45.0 12.5 %all_to_all.22.own_ref = bf16[16,16,384]{2,1,0:T(8,128)(2,1)S(1)} all-to-all(bf16[16,16,384]{2,1,0:T(8,128)(2,1)S(1)} %get-tuple-element.17), channel_id=1, replica_groups=mesh['seq_0'=4,'seq_1'=4,'seq_2'=2,'exp'=8] {'seq_0','seq_1'}, dimensions={0} | all-to-all | bytes 393216 | tf_op jit(solution)/shard_map/all_to_all | solution.py:343
  57.5 0.0 collective-permute-start.2
  57.5 1.4 %collective-permute-done.2.other_ref = bf16[16,16,384]{2,1,0:T(8,128)(2,1)S(1)} collective-permute-done((bf16[16,16,384]{2,1,0:T(8,128)(2,1)S(1)}, bf16[16,16,384]{2,1,0:T(8,128)(2,1)S(1)}, u32[]{:S(2)}, u32[]{:S(2)}) %collective-permute-start.2) | collective-permute-done | bytes 196640 | tf_op jit(solution)/shard_map/ppermute | solution.py:347
  58.9 1.9 %shard_map.131 = (f32[16,32,192]{2,1,0:T(8,128)S(1)}, bf16[17,32,192]{2,1,0:T(8,128)(2,1)S(1)}) custom-call(s32[1,8]{1,0:T(1,128)S(1)} %bitcast.18, bf16[16,16,384]{2,1,0:T(8,128)(2,1)S(1)} %all_to_all.22.own_ref, bf16[16,16,384]{2,1,0:T(8,128)(2,1)S(1)} %collective-permute-done.2.other_ref, f32[16,384]{1,0:T(8,128)S(1)} %get-tuple-element.18.residual_ref, ...), custom_call_target="tpu_custom_call" | custom-call | flops 1048576 | bytes 1048576 | tf_op jit(solution)/shard_map/pallas_call | solution.py:403
  60.8 0.2 collective-permute-start.3
  61.0 1.4 %collective-permute-done.3.got_ref = bf16[17,32,192]{2,1,0:T(8,128)(2,1)S(1)} collective-permute-done((bf16[17,32,192]{2,1,0:T(8,128)(2,1)S(1)}, bf16[17,32,192]{2,1,0:T(8,128)(2,1)S(1)}, u32[]{:S(2)}, u32[]{:S(2)}) %collective-permute-start.3) | collective-permute-done | bytes 208928 | tf_op jit(solution)/shard_map/ppermute | solution.py:347
  62.4 0.4 shard_map.132
  62.8 19.1 %all_to_all.23.in_ref = bf16[128,2,288]{2,1,0:T(2,128)(2,1)S(1)} all-to-all(bf16[128,2,288]{2,1,0:T(2,128)(2,1)S(1)} %shard_map.132), channel_id=1, replica_groups=mesh['seq_0'=4,'seq_1'=4,'seq_2'=2,'exp'=8] {'seq_0','seq_1','exp'}, dimensions={0} | all-to-all | bytes 294912 | tf_op jit(solution)/shard_map/all_to_all | solution.py:343
  81.9 0.9 %shard_map.133 = bf16[3,192]{1,0:T(4,128)(2,1)} custom-call(bf16[128,2,288]{2,1,0:T(2,128)(2,1)S(1)} %all_to_all.23.in_ref, f32[16,384]{1,0:T(8,128)S(1)} %get-tuple-element.18.residual_ref, bf16[17,32,192]{2,1,0:T(8,128)(2,1)S(1)} %collective-permute-done.3.got_ref), custom_call_target="tpu_custom_call" | custom-call | flops 1048576 | bytes 1048576 | tf_op jit(solution)/shard_map/pallas_call | solution.py:412
  (5 shorter events, 0.0 us)
Async XLA Ops:
  0.0 5.1 %copy-start.1 = (bf16[1,6144,256]{2,1,0:T(8,128)(2,1)S(1)}, bf16[1,6144,256]{2,1,0:T(8,128)(2,1)}, u32[]{:S(2)}) copy-start(bf16[1,6144,256]{2,1,0:T(8,128)(2,1)} %ahead_ref.3) | copy-start | bytes 9437188
  0.0 5.1 %collective-permute-start.1 = (bf16[192,768]{1,0:T(8,128)(2,1)}, bf16[192,768]{1,0:T(8,128)(2,1)S(1)}, u32[]{:S(2)}, u32[]{:S(2)}) collective-permute-start(bf16[192,768]{1,0:T(8,128)(2,1)} %bitcast.11), channel_id=1, source_target_pairs={{0,8},{8,0},{1,9},{9,1},{2,10},{10,2},{3,11},{11,3},{4,12},{12,4},... | collective-permute-start | bytes 884744 | tf_op jit(solution)/shard_map/ppermute | solution.py:347
  0.0 25.2 %copy-start.2 = (bf16[1,6144,256]{2,1,0:T(8,128)(2,1)S(1)}, bf16[1,6144,256]{2,1,0:T(8,128)(2,1)}, u32[]{:S(2)}) copy-start(bf16[1,6144,256]{2,1,0:T(8,128)(2,1)} %ahead_ref.4) | copy-start | bytes 9437188
  0.0 25.2 %copy-start.3 = (bf16[768,192]{0,1:T(8,128)(2,1)S(1)}, bf16[768,192]{0,1:T(8,128)(2,1)}, u32[]{:S(2)}) copy-start(bf16[768,192]{0,1:T(8,128)(2,1)} %param.18) | copy-start | bytes 884740
  0.0 25.2 %copy-start.5 = (bf16[3,192]{1,0:T(4,128)(2,1)S(1)}, bf16[3,192]{1,0:T(4,128)(2,1)}, u32[]{:S(2)}) copy-start(bf16[3,192]{1,0:T(4,128)(2,1)} %hidden_ref.3) | copy-start | bytes 3460
  0.0 25.2 %copy-start.7 = (s32[3,2]{0,1:T(2,128)S(1)}, s32[3,2]{0,1:T(2,128)}, u32[]{:S(2)}) copy-start(s32[3,2]{0,1:T(2,128)} %param.21) | copy-start | bytes 76
  3.5 1.6 %collective-permute-start = (f32[128,128]{1,0:T(8,128)S(1)}, f32[128,128]{1,0:T(8,128)S(1)}, u32[]{:S(2)}, u32[]{:S(2)}) collective-permute-start(f32[128,128]{1,0:T(8,128)S(1)} %get-tuple-element.14), channel_id=1, source_target_pairs={{0,8},{8,0},{1,9},{9,1},{2,10},{10,2},{3,11},{11,3},{4,12},{12,4},... | collective-permute-start | bytes 196616 | tf_op jit(solution)/shard_map/ppermute | solution.py:347
  5.4 39.2 %copy-start = (bf16[1,256,6144]{2,1,0:T(8,128)(2,1)S(1)}, bf16[1,256,6144]{2,1,0:T(8,128)(2,1)}, u32[]{:S(2)}) copy-start(bf16[1,256,6144]{2,1,0:T(8,128)(2,1)} %ahead_ref.5) | copy-start | bytes 9437188
  5.4 39.2 %copy-start.4 = (bf16[192,8]{0,1:T(8,128)(2,1)S(1)}, bf16[192,8]{0,1:T(8,128)(2,1)}, u32[]{:S(2)}) copy-start(bf16[192,8]{0,1:T(8,128)(2,1)} %param.20) | copy-start | bytes 9220
  5.4 39.2 %copy-start.6 = (f32[192]{0:T(256)S(1)}, f32[192]{0:T(256)}, u32[]{:S(2)}) copy-start(f32[192]{0:T(256)} %param.19) | copy-start | bytes 2308
  25.2 33.7 %copy-start.8 = (s32[8]{0:T(128)S(1)}, s32[8]{0:T(128)}, u32[]{:S(2)}) copy-start(s32[8]{0:T(128)} %param.22) | copy-start | bytes 100
  57.5 1.4 %collective-permute-start.2 = (bf16[16,16,384]{2,1,0:T(8,128)(2,1)S(1)}, bf16[16,16,384]{2,1,0:T(8,128)(2,1)S(1)}, u32[]{:S(2)}, u32[]{:S(2)}) collective-permute-start(bf16[16,16,384]{2,1,0:T(8,128)(2,1)S(1)} %all_to_all.22.own_ref), channel_id=1, source_target_pairs={{0,8},{8,0},{1,9},{9,1},{2,10},{10,2},{3,11},{11,3},{4,12},{12,4},... | collective-permute-start | bytes 589832 | tf_op jit(solution)/shard_map/ppermute | solution.py:347
  60.8 1.6 %collective-permute-start.3 = (bf16[17,32,192]{2,1,0:T(8,128)(2,1)S(1)}, bf16[17,32,192]{2,1,0:T(8,128)(2,1)S(1)}, u32[]{:S(2)}, u32[]{:S(2)}) collective-permute-start(bf16[17,32,192]{2,1,0:T(8,128)(2,1)S(1)} %get-tuple-element.20), channel_id=1, source_target_pairs={{0,8},{8,0},{1,9},{9,1},{2,10},{10,2},{3,11},{11,3},{4,12},{12,4},... | collective-permute-start | bytes 626696 | tf_op jit(solution)/shard_map/ppermute | solution.py:347

commit v6 on v5

--- a/solution.py
+++ b/solution.py
@@ -313,7 +313,10 @@
     total = jnp.zeros((OWNED, COLS), f32)
     for q in range(4):
         total += jnp.where(me % 4 == q, residual[OWNED * q : OWNED * (q + 1), :], 0.0)
-    experts = jnp.sum(in_ref[...].astype(f32), axis=0)
+    parts = [jnp.sum(in_ref[CHIPS * i : CHIPS * (i + 1)].astype(f32), axis=0) for i in range(EXPERTS)]
+    while len(parts) > 1:
+        parts = [x + y for x, y in zip(parts[::2], parts[1::2])]
+    experts = parts[0]
     last = jnp.concatenate([experts[:1, COLS:], experts[1:, COLS:]], axis=1)
     out_ref[...] = (total + jnp.concatenate([experts[:, :COLS], last], axis=0)).astype(bf16)
 

time: 83 us -> 82.9 us (level)
  no operation moved by 1% of the time
where the time goes in v6:
time: 82.9 us; the launch traced here: 82.7 us
  blocking collectives  69.7 us (84%)
  Pallas kernels  8.16 us (10%)
  waiting for transfers between devices  3.76 us (5%)
  starting transfers between devices  0.91 us (1%)
    all_to_all x4, blocking collectives, exchanged(): return lax.all_to_all(value, axes, 0, 0, tiled=True)  69.7 us
    ppermute x4, waiting for transfers between devices, swapped(): return lax.ppermute(value, 'seq_2', [(0, 1), (1, 0)])  3.76 us
    pallas_call x1, Pallas kernels, on_device(): call(attention_kernel, (shaped((HALF_ROWS, 128), f32), shaped((HALF_ROWS...  3.44 us
    pallas_call x1, Pallas kernels, on_device(): call(expert_kernel, (shaped((CHIPS, 2 * ROWS, COLS), f32), shaped((CHIPS...  1.87 us
  transfers between devices with their start and end apart: 4, of which 3 were waited for; matrix products, arithmetic and copies ran while one was open for 0% of the time, Pallas kernels for 4%

profile of v6, /device:TPU:32, one launch (start us, length us, event | category | flops | bytes accessed | tf_op | source)
XLA Modules:
  0.0 82.7 jit_solution(16300850257469279968)
XLA Ops:
  0.0 0.0 collective-permute-start.1
  0.0 0.0 copy-start.3
  0.0 0.0 copy-start.5
  0.0 0.0 copy-start.7
  0.0 3.4 %shard_map.127 = (f32[96,128]{1,0:T(8,128)S(1)}, f32[128,128]{1,0:T(8,128)S(1)}) custom-call(s32[24]{0:T(128)} %lengths_ref.1, bf16[24,768]{1,0:T(8,128)(2,1)} %q_ref.1, bf16[24,256,128]{2,1,0:T(8,128)(2,1)} %k_ref.1, bf16[24,256,128]{2,1,0:T(8,128)(2,1)} %v_ref.1, bf16[3,192]{1,0:T(4,128)(2,1)} %hidden_ref.3, bf16[8,192]{1,0:T(8,128)(2,1)} %bitcast.13, ...), custom_call_target="tpu_custom_call" | custom-call | flops 1048576 | bytes 1048576 | tf_op jit(solution)/shard_map/pallas_call | solution.py:368
  3.5 0.7 collective-permute-start
  4.2 0.9 %collective-permute-done.got_ref = f32[128,128]{1,0:T(8,128)S(1)} collective-permute-done((f32[128,128]{1,0:T(8,128)S(1)}, f32[128,128]{1,0:T(8,128)S(1)}, u32[]{:S(2)}, u32[]{:S(2)}) %collective-permute-start) | collective-permute-done | bytes 65568 | tf_op jit(solution)/shard_map/ppermute | solution.py:350
  5.1 0.0 collective-permute-done.1.weight_ref.other_ref
  5.1 0.0 copy-done.1
  5.1 0.3 shard_map.128
  5.4 0.0 copy-start
  5.4 0.0 copy-start.4
  5.4 0.0 copy-start.6
  5.4 19.8 %all_to_all.20.in_ref = bf16[16,80,128]{2,1,0:T(8,128)(2,1)S(1)} all-to-all(bf16[16,80,128]{2,1,0:T(8,128)(2,1)S(1)} %shard_map.128), channel_id=1, replica_groups=mesh['seq_0'=4,'seq_1'=4,'seq_2'=2,'exp'=8] {'seq_0','seq_1'}, dimensions={0} | all-to-all | bytes 655360 | tf_op jit(solution)/shard_map/all_to_all | solution.py:346
  25.2 0.0 copy-done.2
  25.2 0.0 copy-done.3
  25.2 0.0 copy-done.5
  25.2 0.0 copy-done.7
  25.2 0.0 copy-start.8
  25.2 1.0 %shard_map.129 = (bf16[8,16,384]{2,1,0:T(8,128)(2,1)S(1)}, f32[16,384]{1,0:T(8,128)S(1)}) custom-call(s32[2,3]{1,0:T(2,128)S(1)} %bitcast.17, bf16[16,80,128]{2,1,0:T(8,128)(2,1)S(1)} %all_to_all.20.in_ref, bf16[3,192]{1,0:T(4,128)(2,1)S(1)} %copy-done.5, f32[128,128]{1,0:T(8,128)S(1)} %collective-permute-done.got_ref, bf16[192,768]{1,0:T(8,128)(2,1)S(1)} %bitcast.12, ...), custom_call_target="tpu_custom_call" | custom-call | flops 1048576 | bytes 1048576 | tf_op jit(solution)/shard_map/pallas_call | solution.py:391
  26.2 18.4 %all_to_all.21.in_ref = bf16[8,16,384]{2,1,0:T(8,128)(2,1)S(1)} all-to-all(bf16[8,16,384]{2,1,0:T(8,128)(2,1)S(1)} %get-tuple-element.15), channel_id=1, replica_groups=mesh['seq_0'=4,'seq_1'=4,'seq_2'=2,'exp'=8] {'exp'}, dimensions={0} | all-to-all | bytes 196608 | tf_op jit(solution)/shard_map/all_to_all | solution.py:346
  44.5 0.0 copy-done
  44.5 0.4 shard_map.130
  45.0 12.5 %all_to_all.22.own_ref = bf16[16,16,384]{2,1,0:T(8,128)(2,1)S(1)} all-to-all(bf16[16,16,384]{2,1,0:T(8,128)(2,1)S(1)} %get-tuple-element.17), channel_id=1, replica_groups=mesh['seq_0'=4,'seq_1'=4,'seq_2'=2,'exp'=8] {'seq_0','seq_1'}, dimensions={0} | all-to-all | bytes 393216 | tf_op jit(solution)/shard_map/all_to_all | solution.py:346
  57.5 0.0 collective-permute-start.2
  57.5 1.4 %collective-permute-done.2.other_ref = bf16[16,16,384]{2,1,0:T(8,128)(2,1)S(1)} collective-permute-done((bf16[16,16,384]{2,1,0:T(8,128)(2,1)S(1)}, bf16[16,16,384]{2,1,0:T(8,128)(2,1)S(1)}, u32[]{:S(2)}, u32[]{:S(2)}) %collective-permute-start.2) | collective-permute-done | bytes 196640 | tf_op jit(solution)/shard_map/ppermute | solution.py:350
  58.9 1.9 %shard_map.131 = (f32[16,32,192]{2,1,0:T(8,128)S(1)}, bf16[17,32,192]{2,1,0:T(8,128)(2,1)S(1)}) custom-call(s32[1,8]{1,0:T(1,128)S(1)} %bitcast.18, bf16[16,16,384]{2,1,0:T(8,128)(2,1)S(1)} %all_to_all.22.own_ref, bf16[16,16,384]{2,1,0:T(8,128)(2,1)S(1)} %collective-permute-done.2.other_ref, f32[16,384]{1,0:T(8,128)S(1)} %get-tuple-element.18.residual_ref, ...), custom_call_target="tpu_custom_call" | custom-call | flops 1048576 | bytes 1048576 | tf_op jit(solution)/shard_map/pallas_call | solution.py:406
  60.8 0.2 collective-permute-start.3
  61.0 1.4 %collective-permute-done.3.got_ref = bf16[17,32,192]{2,1,0:T(8,128)(2,1)S(1)} collective-permute-done((bf16[17,32,192]{2,1,0:T(8,128)(2,1)S(1)}, bf16[17,32,192]{2,1,0:T(8,128)(2,1)S(1)}, u32[]{:S(2)}, u32[]{:S(2)}) %collective-permute-start.3) | collective-permute-done | bytes 208928 | tf_op jit(solution)/shard_map/ppermute | solution.py:350
  62.4 0.4 shard_map.132
  62.8 19.1 %all_to_all.23.in_ref = bf16[128,2,288]{2,1,0:T(2,128)(2,1)S(1)} all-to-all(bf16[128,2,288]{2,1,0:T(2,128)(2,1)S(1)} %shard_map.132), channel_id=1, replica_groups=mesh['seq_0'=4,'seq_1'=4,'seq_2'=2,'exp'=8] {'seq_0','seq_1','exp'}, dimensions={0} | all-to-all | bytes 294912 | tf_op jit(solution)/shard_map/all_to_all | solution.py:346
  81.9 0.8 shard_map.133
  (5 shorter events, 0.0 us)
Async XLA Ops:
  0.0 5.1 %copy-start.1 = (bf16[1,6144,256]{2,1,0:T(8,128)(2,1)S(1)}, bf16[1,6144,256]{2,1,0:T(8,128)(2,1)}, u32[]{:S(2)}) copy-start(bf16[1,6144,256]{2,1,0:T(8,128)(2,1)} %ahead_ref.3) | copy-start | bytes 9437188
  0.0 5.1 %collective-permute-start.1 = (bf16[192,768]{1,0:T(8,128)(2,1)}, bf16[192,768]{1,0:T(8,128)(2,1)S(1)}, u32[]{:S(2)}, u32[]{:S(2)}) collective-permute-start(bf16[192,768]{1,0:T(8,128)(2,1)} %bitcast.11), channel_id=1, source_target_pairs={{0,8},{8,0},{1,9},{9,1},{2,10},{10,2},{3,11},{11,3},{4,12},{12,4},... | collective-permute-start | bytes 884744 | tf_op jit(solution)/shard_map/ppermute | solution.py:350
  0.0 25.2 %copy-start.2 = (bf16[1,6144,256]{2,1,0:T(8,128)(2,1)S(1)}, bf16[1,6144,256]{2,1,0:T(8,128)(2,1)}, u32[]{:S(2)}) copy-start(bf16[1,6144,256]{2,1,0:T(8,128)(2,1)} %ahead_ref.4) | copy-start | bytes 9437188
  0.0 25.2 %copy-start.3 = (bf16[768,192]{0,1:T(8,128)(2,1)S(1)}, bf16[768,192]{0,1:T(8,128)(2,1)}, u32[]{:S(2)}) copy-start(bf16[768,192]{0,1:T(8,128)(2,1)} %param.18) | copy-start | bytes 884740
  0.0 25.2 %copy-start.5 = (bf16[3,192]{1,0:T(4,128)(2,1)S(1)}, bf16[3,192]{1,0:T(4,128)(2,1)}, u32[]{:S(2)}) copy-start(bf16[3,192]{1,0:T(4,128)(2,1)} %hidden_ref.3) | copy-start | bytes 3460
  0.0 25.2 %copy-start.7 = (s32[3,2]{0,1:T(2,128)S(1)}, s32[3,2]{0,1:T(2,128)}, u32[]{:S(2)}) copy-start(s32[3,2]{0,1:T(2,128)} %param.21) | copy-start | bytes 76
  3.5 1.6 %collective-permute-start = (f32[128,128]{1,0:T(8,128)S(1)}, f32[128,128]{1,0:T(8,128)S(1)}, u32[]{:S(2)}, u32[]{:S(2)}) collective-permute-start(f32[128,128]{1,0:T(8,128)S(1)} %get-tuple-element.14), channel_id=1, source_target_pairs={{0,8},{8,0},{1,9},{9,1},{2,10},{10,2},{3,11},{11,3},{4,12},{12,4},... | collective-permute-start | bytes 196616 | tf_op jit(solution)/shard_map/ppermute | solution.py:350
  5.4 39.2 %copy-start = (bf16[1,256,6144]{2,1,0:T(8,128)(2,1)S(1)}, bf16[1,256,6144]{2,1,0:T(8,128)(2,1)}, u32[]{:S(2)}) copy-start(bf16[1,256,6144]{2,1,0:T(8,128)(2,1)} %ahead_ref.5) | copy-start | bytes 9437188
  5.4 39.2 %copy-start.4 = (bf16[192,8]{0,1:T(8,128)(2,1)S(1)}, bf16[192,8]{0,1:T(8,128)(2,1)}, u32[]{:S(2)}) copy-start(bf16[192,8]{0,1:T(8,128)(2,1)} %param.20) | copy-start | bytes 9220
  5.4 39.2 %copy-start.6 = (f32[192]{0:T(256)S(1)}, f32[192]{0:T(256)}, u32[]{:S(2)}) copy-start(f32[192]{0:T(256)} %param.19) | copy-start | bytes 2308
  25.2 33.7 %copy-start.8 = (s32[8]{0:T(128)S(1)}, s32[8]{0:T(128)}, u32[]{:S(2)}) copy-start(s32[8]{0:T(128)} %param.22) | copy-start | bytes 100
  57.5 1.4 %collective-permute-start.2 = (bf16[16,16,384]{2,1,0:T(8,128)(2,1)S(1)}, bf16[16,16,384]{2,1,0:T(8,128)(2,1)S(1)}, u32[]{:S(2)}, u32[]{:S(2)}) collective-permute-start(bf16[16,16,384]{2,1,0:T(8,128)(2,1)S(1)} %all_to_all.22.own_ref), channel_id=1, source_target_pairs={{0,8},{8,0},{1,9},{9,1},{2,10},{10,2},{3,11},{11,3},{4,12},{12,4},... | collective-permute-start | bytes 589832 | tf_op jit(solution)/shard_map/ppermute | solution.py:350
  60.8 1.6 %collective-permute-start.3 = (bf16[17,32,192]{2,1,0:T(8,128)(2,1)S(1)}, bf16[17,32,192]{2,1,0:T(8,128)(2,1)S(1)}, u32[]{:S(2)}, u32[]{:S(2)}) collective-permute-start(bf16[17,32,192]{2,1,0:T(8,128)(2,1)S(1)} %get-tuple-element.20), channel_id=1, source_target_pairs={{0,8},{8,0},{1,9},{9,1},{2,10},{10,2},{3,11},{11,3},{4,12},{12,4},... | collective-permute-start | bytes 626696 | tf_op jit(solution)/shard_map/ppermute | solution.py:350
